TPU v7x, 128 devices: a whole 4x4x4 slice. The times are simulated.
128 devices in a mesh: genes: 64 (over x, z, y), batch: 2 (over core).
Axes of the slice: x: 4, y: 4, z: 4, core: 2. Of those that a mesh axis runs over, the one named last changes fastest.
Arguments:
- genotypes: bfloat16 [256, 3145728], P('batch', 'genes'), may hold values from 0 to 2, as said below
- gene_weight: bfloat16 [16, 3145728], P(None, 'genes'), may hold values from -0.375 to 0.375
- gene_lengths: int32 [12288], P('genes'), may hold values from 128 to 384, as said below
- membership: int32 [12288, 2], replicated, may hold values from 0 to 2047, as said below
- pathway_slot: int32 [2048], replicated, may hold values from 0 to 2047, as said below
- pathway_weight: bfloat16 [24576, 1024], P('genes'), may hold values from -0.4375 to 0.4375
- head_weight: bfloat16 [131072], P('genes'), may hold values from -0.75 to 0.75
- cotangent: float32 [256], P('batch'), may hold values from -3 to 3
Outputs:
- grad_gene: float32 [16, 3145728], P(None, 'genes')
- grad_pathway: float32 [24576, 1024], P('genes')
- grad_head: float32 [131072], P('genes')
Inputs may be any that keep to these rules, and one draw needn't show every extreme that they name: `genotypes`: dosages 0, 1 or 2. `gene_lengths`: the 192 genes of each index of genes together hold exactly its 49152 variants. `membership`: the 2 pathways of a gene differ; of the links of one index's genes at most 12 go to pathways whose slots lie in one index's range of 32 slots, and some index receives exactly 12 from every index. `pathway_slot`: a permutation of the pathways; slot s is held by index s // 32 of genes.
All inputs are finite; a program needn't handle non-finite values.
Results may differ from a plain program's by a relative error of at most 0.0062.
Values may be sent and summed in bfloat16 or wider, within the bound.
A program may use at most 128 MiB of HBM per device.

v0:
```python
import jax
import jax.numpy as jnp
from jax import lax
from jax.sharding import PartitionSpec as P

GLEN = 256


block_cols = 512


def gene_window_count():
    return block_cols // (GLEN // 2) + 2


def gene_windows(lengths, var_count, window):
    starts = jnp.cumsum(lengths) - lengths
    blocks = var_count // block_cols
    block_start = jnp.arange(blocks) * block_cols
    first_gene = jnp.sum((starts[None, :] <= block_start[:, None]).astype(jnp.int32), axis=1) - 1
    padded = jnp.concatenate([starts, jnp.full((window,), var_count, jnp.int32)])
    upcoming = padded[first_gene[:, None] + jnp.arange(1, window, dtype=jnp.int32)[None, :]]
    position = block_start[:, None] + jnp.arange(block_cols, dtype=jnp.int32)[None, :]
    which = jnp.sum((upcoming[:, None, :] <= position[:, :, None]).astype(jnp.int32), axis=2)
    select = which[:, None, :] == jnp.arange(window, dtype=jnp.int32)[None, :, None]
    gene_ids = first_gene[:, None] + jnp.arange(window, dtype=jnp.int32)[None, :]
    return (gene_ids, select)


def contract_first(left, right):
    return lax.dot_general(
        left, right, (((0,), (0,)), ((), ())), preferred_element_type=jnp.float32
    )


def gene_forward(genotype_rows, weight_rows, lengths):
    samples, var_count = genotype_rows.shape
    unit_count = weight_rows.shape[0]
    gene_count = lengths.shape[0]
    window_genes = gene_window_count()
    gene_ids, select = gene_windows(lengths, var_count, window_genes)
    blocks = var_count // block_cols
    rows = genotype_rows.reshape(samples, blocks, block_cols)
    weight_blocks = weight_rows.reshape(unit_count, blocks, block_cols).transpose(1, 0, 2)
    basis = jnp.where(
        select[:, :, None, :], weight_blocks[:, None, :, :], jnp.zeros((), weight_rows.dtype)
    )
    basis = basis.reshape(blocks, window_genes * unit_count, block_cols)
    partial_sums = jnp.einsum("bkv,kcv->kcb", rows, basis, preferred_element_type=jnp.float32)
    partial_sums = partial_sums.reshape(blocks * window_genes, unit_count * samples)
    gene_table = (
        gene_ids.reshape(-1)[None, :] == jnp.arange(gene_count, dtype=jnp.int32)[:, None]
    ).astype(jnp.float32)
    preact = jnp.dot(
        gene_table,
        partial_sums,
        precision=lax.Precision.HIGHEST,
        preferred_element_type=jnp.float32,
    )
    return (preact.reshape(gene_count, unit_count, samples), gene_ids, select)


def gene_backward(genotype_rows, preact_delta, gene_ids, select):
    samples, var_count = genotype_rows.shape
    gene_count, unit_count, _ = preact_delta.shape
    blocks = var_count // block_cols
    window = gene_ids.shape[1]
    rows = genotype_rows.reshape(samples, blocks, block_cols)
    clipped_ids = jnp.minimum(gene_ids, gene_count - 1).reshape(-1)
    window_table = (
        clipped_ids[:, None] == jnp.arange(gene_count, dtype=jnp.int32)[None, :]
    ).astype(jnp.bfloat16)
    windowed = jnp.dot(
        window_table,
        preact_delta.reshape(gene_count, unit_count * samples),
        preferred_element_type=jnp.float32,
    ).astype(jnp.bfloat16)
    windowed = windowed.reshape(blocks, window * unit_count, samples)
    full_terms = jnp.einsum("bkv,kcb->kcv", rows, windowed, preferred_element_type=jnp.float32)
    full_terms = full_terms.reshape(blocks, window, unit_count, block_cols)
    selected_entries = jnp.sum(
        jnp.where(select[:, :, None, :], full_terms, jnp.zeros((), jnp.float32)), axis=1
    )
    return selected_entries.transpose(1, 0, 2).reshape(unit_count, var_count)


def head_step(pathway_sum, head_rows, sample_grad):
    active = jnp.tanh(pathway_sum)
    grad_head = jnp.sum(active * sample_grad[None, None, :], axis=2).reshape(-1)
    pathway_delta = (
        sample_grad[None, None, :] * head_rows[:, :, None] * (1.0 - active * active)
    ).astype(jnp.bfloat16)
    return (grad_head, pathway_delta)


def on_device(
    genotypes,
    gene_weight,
    gene_lengths,
    membership,
    pathway_slot,
    pathway_weight,
    head_weight,
    cotangent,
):
    devices = lax.axis_size("genes")
    own_index = lax.axis_index("genes")
    gene_count = gene_lengths.shape[0]
    edge_count = pathway_weight.shape[0]
    link_count = edge_count // gene_count
    unit_count = gene_weight.shape[0]
    path_units = pathway_weight.shape[1] // unit_count
    owned_paths = head_weight.shape[0] // path_units
    capacity = 2 * edge_count // devices
    samples = genotypes.shape[0]
    total_slots = devices * capacity
    preact, gene_ids, select = gene_forward(genotypes, gene_weight, gene_lengths)
    hidden = jnp.tanh(preact).astype(jnp.bfloat16)
    slot_all = jnp.take(pathway_slot, membership.reshape(-1))
    target_all = slot_all // owned_paths
    own_slots = lax.dynamic_slice_in_dim(slot_all, own_index * edge_count, edge_count)
    own_target = own_slots // owned_paths
    edge_pos = jnp.arange(edge_count, dtype=jnp.int32)
    earlier = edge_pos[None, :] < edge_pos[:, None]
    same_owner = own_target[None, :] == own_target[:, None]
    send_rank = jnp.sum((earlier & same_owner).astype(jnp.int32), axis=1)
    send_place = own_target * capacity + send_rank
    place_table = (send_place[None, :] == jnp.arange(total_slots, dtype=jnp.int32)[:, None]).astype(
        jnp.bfloat16
    )
    arrive = (target_all.reshape(devices, edge_count) == own_index).astype(jnp.int32)
    arrive_rank = jnp.cumsum(arrive, axis=1) - arrive
    local_path = (slot_all % owned_paths).reshape(devices, edge_count)
    hits = (arrive[:, :, None] > 0) & (
        arrive_rank[:, :, None] == jnp.arange(capacity, dtype=jnp.int32)[None, None, :]
    )
    recv_local = jnp.sum(jnp.where(hits, local_path[:, :, None], 0), axis=1)
    filled = jnp.any(hits, axis=1)
    recv_path = jnp.where(filled, recv_local, owned_paths).reshape(-1)
    pick_rows = (recv_path[None, :] == jnp.arange(owned_paths, dtype=jnp.int32)[:, None]).astype(
        jnp.bfloat16
    )
    link_rows = pathway_weight.reshape(edge_count, unit_count, path_units)
    hidden_links = jnp.repeat(hidden, link_count, axis=0)
    head_rows = head_weight.reshape(owned_paths, path_units).astype(jnp.float32)
    message = jnp.einsum(
        "eub,euk->ekb", hidden_links, link_rows, preferred_element_type=jnp.float32
    ).astype(jnp.bfloat16)
    outgoing = jnp.dot(
        place_table,
        message.reshape(edge_count, path_units * samples),
        preferred_element_type=jnp.float32,
    ).astype(jnp.bfloat16)
    incoming_links = lax.all_to_all(
        outgoing.reshape(devices, capacity, path_units, samples),
        "genes",
        split_axis=0,
        concat_axis=0,
        tiled=True,
    )
    pathway_sum = jnp.dot(
        pick_rows,
        incoming_links.reshape(total_slots, path_units * samples),
        preferred_element_type=jnp.float32,
    )
    grad_head, pathway_delta = head_step(
        pathway_sum.reshape(owned_paths, path_units, samples), head_rows, cotangent
    )
    returned = contract_first(
        pick_rows, pathway_delta.reshape(owned_paths, path_units * samples)
    ).astype(jnp.bfloat16)
    replied = lax.all_to_all(
        returned.reshape(devices, capacity, path_units, samples),
        "genes",
        split_axis=0,
        concat_axis=0,
        tiled=True,
    )
    link_delta_rows = contract_first(
        place_table, replied.reshape(total_slots, path_units * samples)
    ).astype(jnp.bfloat16)
    link_delta_rows = link_delta_rows.reshape(edge_count, path_units, samples)
    grad_links = jnp.einsum(
        "eub,ekb->euk", hidden_links, link_delta_rows, preferred_element_type=jnp.float32
    )
    grad_links = grad_links.reshape(edge_count, unit_count * path_units)
    hidden_delta = jnp.einsum(
        "euk,ekb->eub", link_rows, link_delta_rows, preferred_element_type=jnp.float32
    )
    hidden_delta = jnp.sum(
        hidden_delta.reshape(gene_count, link_count, unit_count, samples), axis=1
    )
    latent_broad_matrix = hidden.astype(jnp.float32)
    preact_delta = (hidden_delta * (1.0 - latent_broad_matrix * latent_broad_matrix)).astype(
        jnp.bfloat16
    )
    grad_rows = gene_backward(genotypes, preact_delta, gene_ids, select)
    grad_gene, grad_pathway, grad_head = lax.psum((grad_rows, grad_links, grad_head), "batch")
    return (grad_gene, grad_pathway, grad_head)


def solution(mesh):
    return jax.shard_map(
        on_device,
        mesh=mesh,
        in_specs=(
            P("batch", "genes"),
            P(None, "genes"),
            P("genes"),
            P(),
            P(),
            P("genes", None),
            P("genes"),
            P("batch"),
        ),
        out_specs=(P(None, "genes"), P("genes", None), P("genes")),
        check_vma=False,
    )
```

profile of v0, /device:TPU:1, one launch (start us, length us, event | category | flops | bytes accessed | tf_op | source)
XLA Modules:
  0.0 898.9 jit_solution(5711976715038606374)
XLA Ops:
  12.0 8.9 reshape.381
  20.9 6.1 reshape.380
  38.7 240.6 %gather_fusion.1 = s32[24576]{0:T(1024)} fusion(s32[2048]{0:T(1024)S(1)} %copy-done, s32[24576]{0:T(1024)} %broadcast_clamp_fusion), kind=kCustom, calls=%fused_computation.1 | custom fusion | bytes 294912 | tf_op jit(solution)/shard_map/jit(_take)/gather | solution.py:119
  280.3 5.0 broadcast_select_fusion
  285.3 11.7 %fusion.5 = f32[96,96,128]{2,1,0:T(8,128)} fusion(bf16[96,96,512]{2,1,0:T(8,128)(2,1)} %bitcast.111, bf16[16,96,8,512]{3,2,1,0:T(8,128)(2,1)} %bitcast.109), kind=kOutput, calls=%fused_computation.11 | convolution fusion | flops 1207959552 | bytes 26738688 | tf_op jit(solution)/shard_map/bkv,kcv->kcb/dot_general | solution.py:49
  297.0 5.9 reshape.387
  313.3 12.5 %fusion.14 = bf16[96,8,64,128]{3,1,2,0:T(8,128)(2,1)S(1)} fusion(bf16[48,8,64,128]{3,2,1,0:T(8,128)(2,1)} %bitcast.123, s32[384]{0:T(512)S(1)} %multiply_add_fusion), kind=kOutput, calls=%fused_computation.19 | convolution fusion | flops 4838424576 | bytes 18875904 | tf_op jit(solution)/shard_map/dot_general | solution.py:149
  325.8 6.5 copy.141
  332.3 20.9 %all-to-all-start = ((bf16[64,12,64,128]{3,2,1,0:T(8,128)(2,1)}), bf16[64,12,64,128]{3,2,1,0:T(8,128)(2,1)}, u32[]{:S(2)}, u32[]{:S(2)}) async-start(bf16[64,12,64,128]{3,2,1,0:T(8,128)(2,1)} %bitcast.114), calls=%async_computation | async-start | bytes 25165824 | tf_op jit(solution)/shard_map/all_to_all | solution.py:154
  353.2 5.9 reshape.382
  360.7 6.3 reshape.383
  381.9 149.5 %all-to-all-done = bf16[64,12,64,128]{3,2,1,0:T(8,128)(2,1)} async-done(((bf16[64,12,64,128]{3,2,1,0:T(8,128)(2,1)}), bf16[64,12,64,128]{3,2,1,0:T(8,128)(2,1)}, u32[]{:S(2)}, u32[]{:S(2)}) %all-to-all-start) | async-done | bytes 12582944 | tf_op jit(solution)/shard_map/all_to_all | solution.py:154
  531.4 15.8 %copy.197 = bf16[96,8,64,128]{3,1,2,0:T(8,128)(2,1)} copy(bf16[96,8,64,128]{3,2,1,0:T(8,128)(2,1)} %bitcast.41) | data formatting | bytes 25165824
  547.2 16.6 %copy.123 = bf16[768,8192]{0,1:T(8,128)(2,1)} copy(bf16[768,8192]{1,0:T(8,128)(2,1)} %bitcast.117) | data formatting | bytes 25165824 | tf_op jit(solution)/shard_map/reshape | solution.py:163
  563.8 9.0 multiply_reduce_fusion
  576.4 6.5 copy.143
  582.9 28.6 %all-to-all-start.1 = ((bf16[64,12,64,128]{3,2,1,0:T(8,128)(2,1)}), bf16[64,12,64,128]{3,2,1,0:T(8,128)(2,1)}, u32[]{:S(2)}, u32[]{:S(2)}) async-start(bf16[64,12,64,128]{3,2,1,0:T(8,128)(2,1)} %bitcast.115), calls=%async_computation.1 | async-start | bytes 25165824 | tf_op jit(solution)/shard_map/all_to_all | solution.py:172
  611.6 172.0 %all-to-all-done.1 = bf16[64,12,64,128]{3,2,1,0:T(8,128)(2,1)} async-done(((bf16[64,12,64,128]{3,2,1,0:T(8,128)(2,1)}), bf16[64,12,64,128]{3,2,1,0:T(8,128)(2,1)}, u32[]{:S(2)}, u32[]{:S(2)}) %all-to-all-start.1) | async-done | bytes 12582944 | tf_op jit(solution)/shard_map/all_to_all | solution.py:172
  783.6 11.3 %fusion.21 = bf16[48,8,64,128]{3,1,2,0:T(8,128)(2,1)S(1)} fusion(bf16[96,8,64,128]{3,2,1,0:T(8,128)(2,1)} %bitcast.47, s32[384]{0:T(512)S(1)} %multiply_add_fusion), kind=kOutput, calls=%fused_computation.26 | convolution fusion | flops 4835278848 | bytes 18875904 | tf_op jit(solution)/shard_map/dot_general | solution.py:31
  796.8 5.1 fusion.58
  818.2 13.7 %fusion.3 = f32[96,96,512]{2,1,0:T(8,128)} fusion(bf16[96,96,128]{2,1,0:T(8,128)(2,1)S(1)} %reshape.399, bf16[16,96,8,512]{3,2,1,0:T(8,128)(2,1)} %bitcast.110), kind=kOutput, calls=%fused_computation.9 | convolution fusion | flops 1207959552 | bytes 33816576 | tf_op jit(solution)/shard_map/bkv,kcb->kcv/dot_general | solution.py:79
  831.9 8.4 select_reduce_fusion
  842.5 6.0 psum.23
  848.5 38.3 %all-reduce.5.cloned.1.call-done = (f32[16,49152]{1,0:T(8,128)}, f32[384,1024]{0,1:T(8,128)}) async-done(((f32[16,49152]{1,0:T(8,128)}, f32[384,1024]{0,1:T(8,128)}), (f32[16,49152]{1,0:T(8,128)}, f32[384,1024]{0,1:T(8,128)})) %all-reduce.5.cloned.1.call-update) | async-done | bytes 4718608 | tf_op jit(solution)/shard_map/psum | solution.py:198
  (87 shorter events, 73.2 us)
Async XLA Ops:
  7.2 31.6 %copy-start = (s32[2048]{0:T(1024)S(1)}, s32[2048]{0:T(1024)}, u32[]{:S(2)}) copy-start(s32[2048]{0:T(1024)} %param.12) | copy-start | bytes 24580
  20.9 6.1 copy-start.8
  28.3 4.3 copy-start.5
  307.8 0.9 copy-start.3
  332.3 199.0 %all-to-all-start = ((bf16[64,12,64,128]{3,2,1,0:T(8,128)(2,1)}), bf16[64,12,64,128]{3,2,1,0:T(8,128)(2,1)}, u32[]{:S(2)}, u32[]{:S(2)}) async-start(bf16[64,12,64,128]{3,2,1,0:T(8,128)(2,1)} %bitcast.114), calls=%async_computation | async-start | bytes 25165824 | tf_op jit(solution)/shard_map/all_to_all | solution.py:154
  359.1 9.5 %copy-start.7 = (bf16[2048]{0:T(1024)(128)(2,1)S(1)}, bf16[2048]{0:T(1024)(128)(2,1)}, u32[]{:S(2)}) copy-start(bf16[2048]{0:T(1024)(128)(2,1)} %param.14) | copy-start | bytes 12292
  547.2 16.6 %copy-start.9 = (f32[128]{0:T(128)S(1)}, f32[128]{0:T(128)}, u32[]{:S(2)}) copy-start(f32[128]{0:T(128)} %param.15) | copy-start | bytes 1540
  582.9 200.7 %all-to-all-start.1 = ((bf16[64,12,64,128]{3,2,1,0:T(8,128)(2,1)}), bf16[64,12,64,128]{3,2,1,0:T(8,128)(2,1)}, u32[]{:S(2)}, u32[]{:S(2)}) async-start(bf16[64,12,64,128]{3,2,1,0:T(8,128)(2,1)} %bitcast.115), calls=%async_computation.1 | async-start | bytes 25165824 | tf_op jit(solution)/shard_map/all_to_all | solution.py:172
  611.5 275.2 %all-reduce.5.cloned.1.call-start = ((), (), s32[]{:S(2)}) async-start(), calls=%async_computation.2 | async-start | bytes 9437184 | tf_op jit(solution)/shard_map/psum | solution.py:198
  805.3 3.4 copy-start.2
  840.3 2.0 copy-start.6
  886.7 3.2 copy-start.4
  886.7 4.8 copy-start.1
Sparse Core Ops, SparseCore 0:
  842.5 44.2 all-reduce.4
where the time goes:
time: 909 us; the launch traced here: 899 us
  waiting for transfers between devices  360 us (40%)
  local copies, waits for them, and re-layouts  359 us (39%)
  matrix products  83.1 us (9%)
  starting transfers between devices  49.5 us (5%)
  other arithmetic  26.7 us (3%)
  between operations  14.8 us (2%)
    gather x3, local copies, waits for them, and re-layouts, on_device(): slot_all = jnp.take(pathway_slot, membership.reshape(-1))  244 us
    all_to_all x1, waiting for transfers between devices, on_device(): lax.all_to_all(returned.reshape(devices, capacity, path_units, samples),...  172 us
    all_to_all x1, waiting for transfers between devices, on_device(): lax.all_to_all(outgoing.reshape(devices, capacity, path_units, samples),...  149 us
    unnamed x29, local copies, waits for them, and re-layouts  43.5 us
    psum x1, waiting for transfers between devices, on_device(): lax.psum((grad_rows, grad_links, grad_head), 'batch')  38.3 us
    all_to_all x1, starting transfers between devices, on_device(): lax.all_to_all(returned.reshape(devices, capacity, path_units, samples),...  28.6 us
    reshape x4, local copies, waits for them, and re-layouts, on_device(): slot_all = jnp.take(pathway_slot, membership.reshape(-1))  27.2 us
    all_to_all x1, starting transfers between devices, on_device(): lax.all_to_all(outgoing.reshape(devices, capacity, path_units, samples),...  20.9 us
  transfers between devices with their start and end apart: 3, of which 3 were waited for; matrix products, arithmetic and copies ran while one was open for 3% of the time, Pallas kernels for 0%

commit v1 on v0

v1 whole, which is shorter than its diff:
```python
import functools

import jax
import jax.numpy as jnp
from jax import lax
from jax.experimental import pallas as pl
from jax.experimental.pallas import tpu as pltpu
from jax.sharding import PartitionSpec as P

MESH = pl.DeviceIdType.MESH
F32 = jnp.float32
BF16 = jnp.bfloat16
I32 = jnp.int32

CAP = 12
HALF = CAP // 2
COLS = 256
STEP = 2048
GROUP = 32
MAX_GROUPS = 56
STRIDE = 27

ROW_SEND = 0
ROW_PERM = 12
ROW_SLOT = 26
ROW_RET = 28
ROW_START = 32
ROW_FIRST = 34
TAB_ROWS = 40


def iota(shape, dim):
    return lax.broadcasted_iota(I32, shape, dim)


def one(mask):
    return jnp.where(mask, 1.0, 0.0).astype(BF16)


def mm(left, right):
    return jnp.dot(left, right, preferred_element_type=F32)


def mm_tn(left, right):
    return lax.dot_general(left, right, (((0,), (0,)), ((), ())), preferred_element_type=F32)


def mm_nt(left, right):
    return lax.dot_general(left, right, (((1,), (1,)), ((), ())), preferred_element_type=F32)


def to_col(row, n):
    eye = iota((n, n), 0) == iota((n, n), 1)
    return jnp.sum(jnp.where(eye, jnp.broadcast_to(row, (n, n)), 0.0), axis=1, keepdims=True)


def to_row(col, n):
    eye = iota((n, n), 0) == iota((n, n), 1)
    return jnp.sum(jnp.where(eye, jnp.broadcast_to(col, (n, n)), 0.0), axis=0, keepdims=True)


def index_kernel(devs, genes, paths, mem_ref, slot_ref, len_ref, tab_ref, s_ref, own_ref):
    me = lax.axis_index("genes")
    per = genes
    table = slot_ref[...]
    halves = jnp.concatenate([table >> 5, table & 31], axis=0).astype(F32).astype(BF16)
    rows = table.shape[0]
    pair = 2 * per

    for m in range(2):
        def look(j, _, m=m):
            q = mem_ref[m : m + 1, pl.ds(pl.multiple_of(j * pair, 128), pair)]
            lane = q & 127
            which = q >> 7
            hot = one(jnp.broadcast_to(lane, (128, pair)) == iota((128, pair), 0))
            vals = mm(halves, hot)
            pick = jnp.broadcast_to(which, (rows, pair)) == iota((rows, pair), 0)
            owner = jnp.sum(jnp.where(pick, vals[:rows], 0.0), axis=0, keepdims=True)
            local = jnp.sum(jnp.where(pick, vals[rows:], 0.0), axis=0, keepdims=True)
            slot = owner * 32.0 + local
            s_ref[pl.ds(m * devs + 2 * j, 1), :] = slot[:, :per]
            s_ref[pl.ds(m * devs + 2 * j + 1, 1), :] = slot[:, per:]
            return 0

        lax.fori_loop(0, devs // 2, look, 0, unroll=4)

    tab_ref[...] = jnp.zeros((TAB_ROWS, 128), I32)
    slots = s_ref[...].astype(I32)
    mine = (slots >> 5) == me
    local = (slots & 31).astype(F32)
    upper = one(iota((per, per), 0) < iota((per, per), 1))
    before = mm(one(mine), upper)
    count = jnp.sum(jnp.where(mine, 1.0, 0.0), axis=1, keepdims=True)
    lead = jnp.concatenate([jnp.zeros((devs, 1), F32), count[:devs]], axis=0)
    rank = before + lead
    lower = one(iota((devs, devs), 1) < iota((devs, devs), 0))
    lane64 = iota((devs, 128), 1)
    carry = jnp.zeros((1, 128), F32)
    places, cells = [], []
    for r in range(CAP):
        hit = mine & (rank == float(r))
        got = jnp.sum(jnp.where(hit, local + 1.0, 0.0), axis=1, keepdims=True)
        got = got[:devs] + got[devs:]
        cell = jnp.where(got == 0.0, float(paths), got - 1.0).astype(I32)
        hot = jnp.broadcast_to(cell, (devs, 128)) == lane64
        within = mm(lower, one(hot)) + carry
        carry = carry + jnp.sum(jnp.where(hot, 1.0, 0.0), axis=0, keepdims=True)
        places.append(jnp.sum(jnp.where(hot, within, 0.0), axis=1, keepdims=True))
        cells.append(hot)
    lane1 = iota((1, 128), 1)
    groups = jnp.where(lane1 < paths, ((carry.astype(I32) + (GROUP - 1)) // GROUP).astype(F32), 0.0)
    strict = one(iota((128, 128), 0) < iota((128, 128), 1))
    start = mm(jnp.broadcast_to(groups.astype(BF16), (8, 128)), strict)[:1]
    end_col = to_col(start + groups, 128)
    ends = jnp.where(
        (jnp.broadcast_to(end_col, (128, 128)) <= iota((128, 128), 1).astype(F32))
        & (iota((128, 128), 0) < paths),
        1.0,
        0.0,
    )
    tab_ref[ROW_SLOT : ROW_SLOT + 1, :] = jnp.sum(ends, axis=0, keepdims=True).astype(I32)
    total = jnp.sum(groups, axis=1, keepdims=True)
    tab_ref[ROW_SLOT + 1 : ROW_SLOT + 2, :] = jnp.broadcast_to(total, (1, 128)).astype(I32)
    src_sum = jnp.zeros((16, 128), F32)
    rank_sum = jnp.zeros((16, 128), F32)
    seen = jnp.zeros((16, 128), F32)
    source = iota((devs, 128), 0).astype(F32).astype(BF16)
    for r in range(CAP):
        first = jnp.sum(
            jnp.where(cells[r], jnp.broadcast_to(start, (devs, 128)), 0.0), axis=1, keepdims=True
        )
        real = jnp.sum(jnp.where(cells[r] & (lane64 < paths), 1.0, 0.0), axis=1, keepdims=True)
        pos = (first * float(GROUP) + places[r]).astype(I32)
        pos = jnp.where(real > 0.0, pos, 1 << 20)
        high = one(jnp.broadcast_to(pos >> 7, (devs, 16)) == iota((devs, 16), 1))
        low = jnp.broadcast_to(pos & 127, (devs, 128)) == lane64
        src_sum = src_sum + mm_tn(high, jnp.where(low, source, jnp.zeros((), BF16)))
        found = mm_tn(high, one(low))
        rank_sum = rank_sum + found * float(r)
        seen = seen + found
    perm = jnp.where(seen > 0.0, src_sum * float(CAP) + rank_sum, float(devs * CAP))
    tab_ref[ROW_PERM : ROW_PERM + 14, :] = perm.astype(I32)[:14]

    own_ref[0:1, :] = s_ref[pl.ds(me, 1), :]
    own_ref[1:2, :] = s_ref[pl.ds(devs + me, 1), :]
    lower_g = one(iota((per, per), 1) < iota((per, per), 0))
    lane_g = iota((per, 128), 1)
    gene_col = iota((per, 128), 0).astype(F32).astype(BF16)
    carry = jnp.zeros((1, 128), F32)
    send = jnp.zeros((16, 128), F32)
    for m in range(2):
        owner = (to_col(own_ref[m : m + 1, :], per).astype(I32)) >> 5
        hot = jnp.broadcast_to(owner, (per, 128)) == lane_g
        within = mm(lower_g, one(hot)) + carry
        carry = carry + jnp.sum(jnp.where(hot, 1.0, 0.0), axis=0, keepdims=True)
        order = jnp.sum(jnp.where(hot, within, 0.0), axis=1, keepdims=True)
        cell = one(jnp.broadcast_to(order, (per, 16)) == iota((per, 16), 1).astype(F32))
        send = send + 2.0 * mm_tn(cell, jnp.where(hot, gene_col, jnp.zeros((), BF16)))
        if m:
            send = send + mm_tn(cell, one(hot))
        back = to_row(owner.astype(F32) * float(CAP) + order, per).astype(I32)
        tab_ref[ROW_RET + 2 * m : ROW_RET + 2 * m + 1, :] = back[:, :128]
        tab_ref[ROW_RET + 2 * m + 1 : ROW_RET + 2 * m + 2, : per - 128] = back[:, 128:]
    tab_ref[ROW_SEND : ROW_SEND + CAP, :] = send.astype(I32)[:CAP]

    lens = len_ref[...].astype(F32) - 128.0
    starts = mm(jnp.broadcast_to(lens.astype(BF16), (8, per)), upper)[:1]
    starts = starts + 128.0 * iota((1, per), 1).astype(F32)
    tab_ref[ROW_START : ROW_START + 1, :] = starts[:, :128].astype(I32)
    var_count = per * COLS
    tab_ref[ROW_START + 1 : ROW_START + 2, :] = jnp.full((1, 128), var_count, I32)
    tab_ref[ROW_START + 1 : ROW_START + 2, : per - 128] = starts[:, 128:].astype(I32)
    start_col = to_col(starts, per)
    begin = (iota((per, 256), 1) * COLS).astype(F32)
    inside = jnp.where(jnp.broadcast_to(start_col, (per, 256)) <= begin, 1.0, 0.0)
    first = (jnp.sum(inside, axis=0, keepdims=True) - 1.0).astype(I32)
    tab_ref[ROW_FIRST : ROW_FIRST + 1, :] = first[:, :128]
    tab_ref[ROW_FIRST + 1 : ROW_FIRST + 2, :] = first[:, 128:]


def look_up(tab_ref, row, index):
    return tab_ref[row + (index >> 7), index & 127]


def window_of(tab_ref, block):
    first = look_up(tab_ref, ROW_FIRST, block)
    one_end = look_up(tab_ref, ROW_START, first + 1) - block * COLS
    two_end = look_up(tab_ref, ROW_START, first + 2) - block * COLS
    return first, one_end, two_end


def forward_kernel(genes, units, tab_ref, geno_ref, weight_ref, hid_ref, acc_ref):
    step = pl.program_id(0)

    @pl.when(step == 0)
    def _():
        acc_ref[...] = jnp.zeros_like(acc_ref)

    pos = iota((units, COLS), 1)
    for k in range(STEP // COLS):
        first, one_end, two_end = window_of(tab_ref, step * (STEP // COLS) + k)
        weight = weight_ref[:, k * COLS : (k + 1) * COLS].astype(F32)
        not_one = pos >= one_end
        not_two = pos >= two_end
        zero = jnp.zeros_like(weight)
        basis = jnp.concatenate(
            [
                jnp.where(not_one, zero, weight),
                jnp.where(not_one & jnp.logical_not(not_two), weight, zero),
                jnp.where(not_two, weight, zero),
            ],
            axis=0,
        ).astype(BF16)
        part = mm_nt(basis, geno_ref[:, k * COLS : (k + 1) * COLS])
        rows = pl.ds(pl.multiple_of(first * units, units), 3 * units)
        acc_ref[rows, :] = acc_ref[rows, :] + part

    @pl.when(step == pl.num_programs(0) - 1)
    def _():
        def finish(g, _):
            base = g * units
            even = acc_ref[pl.ds(base, units // 2, stride=2), :]
            odd = acc_ref[pl.ds(base + 1, units // 2, stride=2), :]
            hid_ref[g] = jnp.tanh(jnp.concatenate([even, odd], axis=1)).astype(BF16)
            return 0

        lax.fori_loop(0, genes, finish, 0, unroll=8)


def partner(me, k):
    off = lax.rem(k * STRIDE, 64)
    x = lax.rem(me // 16 + off // 16, 4)
    z = lax.rem((me // 4) % 4 + (off // 4) % 4, 4)
    y = lax.rem(me % 4 + off % 4, 4)
    return x * 16 + z * 4 + y


def greet(devs, me, core):
    barrier = pltpu.get_barrier_semaphore()

    def hello(k, _):
        pl.semaphore_signal(
            barrier, inc=1, device_id=(partner(me, k), core), device_id_type=MESH
        )
        return 0

    lax.fori_loop(1, devs, hello, 0)
    pl.semaphore_signal(barrier, inc=1, device_id=(me, 1 - core), device_id_type=MESH)
    pl.semaphore_wait(barrier, devs)


def send_kernel(
    devs, tab_ref, hid_ref, link_ref, geno_ref, h_ref, w_ref, sib_ref,
    hs_ref, ws_ref, hsend, hrecv, wsend, wrecv, pair_sem, geno_sem,
):
    me = lax.axis_index("genes")
    core = lax.axis_index("batch")
    low = core * HALF
    greet(devs, me, core)
    geno = pltpu.make_async_remote_copy(
        src_ref=geno_ref, dst_ref=sib_ref, send_sem=geno_sem.at[0], recv_sem=geno_sem.at[1],
        device_id=(me, 1 - core), device_id_type=MESH,
    )
    geno.start()

    def w_copy(k):
        to = partner(me, k)
        return pltpu.make_async_remote_copy(
            src_ref=ws_ref.at[to], dst_ref=w_ref.at[me, pl.ds(low, HALF)],
            send_sem=wsend.at[k], recv_sem=wrecv.at[k],
            device_id=(to, core), device_id_type=MESH,
        )

    def h_copy(k):
        to = partner(me, k)
        return pltpu.make_async_remote_copy(
            src_ref=hs_ref.at[to], dst_ref=h_ref.at[me],
            send_sem=hsend.at[k], recv_sem=hrecv.at[k],
            device_id=(to, core), device_id_type=MESH,
        )

    def w_step(k, _):
        to = partner(me, k)
        for r in range(HALF):
            ws_ref[to, r] = link_ref[tab_ref[low + r, to]]
        w_copy(k).start()
        return 0

    lax.fori_loop(1, devs, w_step, 0)

    def h_step(k, _):
        to = partner(me, k)
        for r in range(CAP):
            hs_ref[to, r] = hid_ref[tab_ref[r, to] >> 1]
        h_copy(k).start()
        return 0

    lax.fori_loop(1, devs, h_step, 0)
    for r in range(CAP):
        h_ref[me, r] = hid_ref[tab_ref[r, me] >> 1]
    for r in range(HALF):
        w_ref[me, low + r] = link_ref[tab_ref[low + r, me]]
    h_ref[devs] = jnp.zeros(h_ref.shape[1:], BF16)
    w_ref[devs] = jnp.zeros(w_ref.shape[1:], BF16)

    def w_wait(k, _):
        w_copy(k).wait()
        return 0

    lax.fori_loop(1, devs, w_wait, 0)
    part = w_ref.at[pl.ds(0, devs), pl.ds(low, HALF)]
    share = pltpu.make_async_remote_copy(
        src_ref=part, dst_ref=part, send_sem=pair_sem.at[0], recv_sem=pair_sem.at[1],
        device_id=(me, 1 - core), device_id_type=MESH,
    )
    share.start()

    def h_wait(k, _):
        h_copy(k).wait()
        return 0

    lax.fori_loop(1, devs, h_wait, 0)
    share.wait()
    geno.wait()


def path_kernel(
    paths, punits, tab_ref, h_ref, w_ref, head_ref, cot_ref, hd_ref, gp_ref, gh_ref,
    hs_ref, ws_ref, sum_ref, delta_ref,
):
    total = tab_ref[ROW_SLOT + 1, 0]
    pairs = (total + 1) // 2
    sum_ref[...] = jnp.zeros_like(sum_ref)
    wide = 8 * GROUP

    def up(i, _):
        for half in range(2):
            c = 2 * i + half
            for j in range(GROUP):
                p = look_up(tab_ref, ROW_PERM, c * GROUP + j)
                hs_ref[c, pl.ds(8 * j, 8), :] = h_ref[p]
                ws_ref[c, pl.ds(8 * j, 8), :] = w_ref[p]
        for half in range(2):
            c = 2 * i + half
            slot = tab_ref[ROW_SLOT, c]
            out = mm_tn(ws_ref[c], hs_ref[c])
            sum_ref[slot] = sum_ref[slot] + out[:punits, :128] + out[punits:, 128:]
        return 0

    lax.fori_loop(0, pairs, up, 0)

    cot = cot_ref[...]
    lane = iota((punits, 128), 1)
    sub = iota((punits, 128), 0)

    def middle(i, _):
        row = jnp.zeros((1, 128), F32)
        head_row = head_ref[pl.ds(i, 1), :]
        for half in range(2):
            s = 2 * i + half
            active = jnp.tanh(sum_ref[s])
            diag = lane == sub + punits * half
            head = jnp.sum(
                jnp.where(diag, jnp.broadcast_to(head_row, (punits, 128)), 0.0),
                axis=1, keepdims=True,
            )
            grad = jnp.sum(active * cot, axis=1, keepdims=True)
            row = row + jnp.sum(
                jnp.where(diag, jnp.broadcast_to(grad, (punits, 128)), 0.0), axis=0, keepdims=True
            )
            delta = (cot * head * (1.0 - active * active)).astype(BF16)
            none = jnp.zeros_like(delta)
            delta_ref[s] = jnp.concatenate(
                [
                    jnp.concatenate([delta, none], axis=1),
                    jnp.concatenate([none, delta], axis=1),
                ],
                axis=0,
            )
        gh_ref[pl.ds(i, 1), :] = row
        return 0

    lax.fori_loop(0, paths // 2, middle, 0)
    delta_ref[paths] = jnp.zeros(delta_ref.shape[1:], BF16)

    def down(i, _):
        for half in range(2):
            c = 2 * i + half
            block = delta_ref[tab_ref[ROW_SLOT, c]]
            hd = mm(ws_ref[c], block).astype(BF16)
            gp = mm_nt(hs_ref[c], block)
            for j in range(GROUP):
                p = look_up(tab_ref, ROW_PERM, c * GROUP + j)
                hd_ref[p] = hd[8 * j : 8 * j + 8]
                gp_ref[p] = gp[8 * j : 8 * j + 8]
        return 0

    lax.fori_loop(0, pairs, down, 0)


def return_kernel(
    devs, genes, units, tab_ref, hd_ref, gp_ref, gh_ref, hid_ref,
    own_ref, sib_ref, link_ref, head_ref,
    back_ref, part_ref, gs_ref, ghs_ref, pd_ref,
    hsend, hrecv, gsend, grecv, pair_sem,
):
    me = lax.axis_index("genes")
    core = lax.axis_index("batch")
    low = core * HALF
    other = (1 - core) * HALF
    greet(devs, me, core)

    def pair(src, dst, n):
        return pltpu.make_async_remote_copy(
            src_ref=src, dst_ref=dst, send_sem=pair_sem.at[2 * n], recv_sem=pair_sem.at[2 * n + 1],
            device_id=(me, 1 - core), device_id_type=MESH,
        )

    def h_copy(k):
        to = partner(me, k)
        return pltpu.make_async_remote_copy(
            src_ref=hd_ref.at[to], dst_ref=back_ref.at[me],
            send_sem=hsend.at[k], recv_sem=hrecv.at[k],
            device_id=(to, core), device_id_type=MESH,
        )

    def g_copy(k):
        to = partner(me, k)
        return pltpu.make_async_remote_copy(
            src_ref=gs_ref.at[to], dst_ref=link_ref.at[me, pl.ds(low, HALF)],
            send_sem=gsend.at[k], recv_sem=grecv.at[k],
            device_id=(to, core), device_id_type=MESH,
        )

    def h_step(k, _):
        h_copy(k).start()
        return 0

    lax.fori_loop(1, devs, h_step, 0)
    parts = pair(gp_ref.at[pl.ds(0, devs), pl.ds(other, HALF)], part_ref, 0)
    parts.start()
    heads = pair(gh_ref, ghs_ref, 1)
    heads.start()
    back_ref[me] = hd_ref[me]
    parts.wait()

    def g_step(k, _):
        to = partner(me, k)
        gs_ref[to] = (gp_ref[to, pl.ds(low, HALF)] + part_ref[to]).astype(BF16)
        g_copy(k).start()
        return 0

    lax.fori_loop(1, devs, g_step, 0)
    link_ref[me, pl.ds(low, HALF)] = (gp_ref[me, pl.ds(low, HALF)] + part_ref[me]).astype(BF16)
    heads.wait()
    head_ref[...] = gh_ref[...] + ghs_ref[...]

    def h_wait(k, _):
        h_copy(k).wait()
        return 0

    lax.fori_loop(1, devs, h_wait, 0)

    def gene(g, _):
        a = look_up(tab_ref, ROW_RET, g)
        b = look_up(tab_ref, ROW_RET + 2, g)
        both = (
            back_ref[a // CAP, a % CAP].astype(F32) + back_ref[b // CAP, b % CAP].astype(F32)
        )
        hid = hid_ref[g].astype(F32)
        value = both * (1.0 - hid * hid)
        base = g * units
        pd_ref[pl.ds(base, units // 2, stride=2), :] = value[:, :128]
        pd_ref[pl.ds(base + 1, units // 2, stride=2), :] = value[:, 128:]
        return 0

    lax.fori_loop(0, genes, gene, 0, unroll=4)
    pad = own_ref.shape[0] - genes * units
    own_ref[pl.ds(0, genes * units), :] = pd_ref[...].astype(BF16)
    own_ref[pl.ds(genes * units, pad), :] = jnp.zeros((pad, 128), BF16)
    deltas = pair(own_ref, sib_ref, 2)
    deltas.start()

    def g_wait(k, _):
        g_copy(k).wait()
        return 0

    lax.fori_loop(1, devs, g_wait, 0)
    mine = link_ref.at[pl.ds(0, devs), pl.ds(low, HALF)]
    share = pair(mine, mine, 3)
    share.start()
    deltas.wait()
    share.wait()


def backward_kernel(
    units, tab_ref, own_ref, sib_ref, pd_own, pd_sib, link_ref, out_ref, gp_ref, gp_scr
):
    step = pl.program_id(0)
    links = gp_ref.shape[0]
    for j in range(links):
        g = step * (links // 2) + j // 2
        p = look_up(tab_ref, ROW_RET + 2 * (j % 2), g)
        gp_scr[pl.ds(8 * j, 8), :] = link_ref[p].astype(F32)
    for e in range(links // 8):
        for t in range(8):
            gp_ref[8 * e : 8 * e + 8, 128 * t : 128 * t + 128] = gp_scr[
                pl.ds(64 * e + t, 8, stride=8), :
            ]
    pos = iota((units, COLS), 1)
    for k in range(STEP // COLS):
        first, one_end, two_end = window_of(tab_ref, step * (STEP // COLS) + k)
        rows = pl.ds(pl.multiple_of(first * units, units), 3 * units)
        left = jnp.concatenate([pd_own[rows, :], pd_sib[rows, :]], axis=1)
        cols = slice(k * COLS, (k + 1) * COLS)
        right = jnp.concatenate([own_ref[:, cols], sib_ref[:, cols]], axis=0)
        full = mm(left, right)
        out_ref[:, cols] = jnp.where(
            pos >= two_end,
            full[2 * units :],
            jnp.where(pos >= one_end, full[units : 2 * units], full[:units]),
        )


def vmem():
    return pl.BlockSpec(memory_space=pltpu.VMEM)


def smem():
    return pl.BlockSpec(memory_space=pltpu.SMEM)


def hbm():
    return pl.BlockSpec(memory_space=pl.ANY)


LIMIT = 60 * 1024 * 1024


def on_device(
    genotypes, gene_weight, gene_lengths, membership, pathway_slot, pathway_weight,
    head_weight, cotangent,
):
    devs = lax.axis_size("genes")
    genes = gene_lengths.shape[0]
    links = pathway_weight.shape[0]
    units = gene_weight.shape[0]
    samples, variants = genotypes.shape
    punits = pathway_weight.shape[1] // units
    paths = head_weight.shape[0] // punits
    half = units // 2
    steps = variants // STEP
    shape = jax.ShapeDtypeStruct

    tab = pl.pallas_call(
        functools.partial(index_kernel, devs, genes, paths),
        out_shape=shape((TAB_ROWS, 128), I32),
        in_specs=[vmem()] * 3,
        out_specs=vmem(),
        scratch_shapes=[pltpu.VMEM((2 * devs, genes), F32), pltpu.VMEM((2, genes), F32)],
        compiler_params=pltpu.CompilerParams(vmem_limit_bytes=LIMIT),
        name="index",
    )(membership.T, pathway_slot.reshape(-1, 128), gene_lengths.reshape(1, -1))

    hidden = pl.pallas_call(
        functools.partial(forward_kernel, genes, units),
        out_shape=shape((genes, half, 2 * samples), BF16),
        grid=(steps,),
        in_specs=[
            smem(),
            pl.BlockSpec((samples, STEP), lambda i: (0, i)),
            pl.BlockSpec((units, STEP), lambda i: (0, i)),
        ],
        out_specs=pl.BlockSpec((genes, half, 2 * samples), lambda i: (0, 0, 0)),
        scratch_shapes=[pltpu.VMEM(((genes + 2) * units, samples), F32)],
        compiler_params=pltpu.CompilerParams(vmem_limit_bytes=LIMIT),
        name="gene_forward",
    )(tab, genotypes, gene_weight)

    link_rows = pathway_weight.reshape(links, half, 2 * punits)
    got_hidden, got_links, sibling = pl.pallas_call(
        functools.partial(send_kernel, devs),
        out_shape=(
            shape((devs + 1, CAP, half, 2 * samples), BF16),
            shape((devs + 1, CAP, half, 2 * punits), BF16),
            shape((samples, variants), BF16),
        ),
        in_specs=[smem(), vmem(), vmem(), hbm()],
        out_specs=(vmem(), vmem(), hbm()),
        scratch_shapes=[
            pltpu.VMEM((devs, CAP, half, 2 * samples), BF16),
            pltpu.VMEM((devs, HALF, half, 2 * punits), BF16),
        ]
        + [pltpu.SemaphoreType.DMA((devs,))] * 4
        + [pltpu.SemaphoreType.DMA((2,)), pltpu.SemaphoreType.DMA((2,))],
        compiler_params=pltpu.CompilerParams(
            collective_id=0, has_side_effects=True, vmem_limit_bytes=LIMIT
        ),
        name="send_links",
    )(tab, hidden, link_rows, genotypes)

    rows = (devs + 1) * CAP
    deltas, link_parts, head_part = pl.pallas_call(
        functools.partial(path_kernel, paths, punits),
        out_shape=(
            shape((rows, half, 2 * samples), BF16),
            shape((rows, half, 2 * punits), F32),
            shape((paths * punits // 128, 128), F32),
        ),
        in_specs=[smem()] + [vmem()] * 4,
        out_specs=(vmem(),) * 3,
        scratch_shapes=[
            pltpu.VMEM((MAX_GROUPS, 8 * GROUP, 2 * samples), BF16),
            pltpu.VMEM((MAX_GROUPS, 8 * GROUP, 2 * punits), BF16),
            pltpu.VMEM((paths + 1, punits, samples), F32),
            pltpu.VMEM((paths + 1, 2 * punits, 2 * samples), BF16),
        ],
        compiler_params=pltpu.CompilerParams(vmem_limit_bytes=LIMIT),
        name="pathways",
    )(
        tab,
        got_hidden.reshape(rows, half, 2 * samples),
        got_links.reshape(rows, half, 2 * punits),
        head_weight.astype(F32).reshape(-1, 128),
        cotangent.reshape(1, -1),
    )

    pad_rows = (genes + 2) * units
    own, sib, got_parts, grad_head = pl.pallas_call(
        functools.partial(return_kernel, devs, genes, units),
        out_shape=(
            shape((pad_rows, samples), BF16),
            shape((pad_rows, samples), BF16),
            shape((devs, CAP, half, 2 * punits), BF16),
            shape(head_part.shape, F32),
        ),
        in_specs=[smem()] + [vmem()] * 4,
        out_specs=(vmem(),) * 4,
        scratch_shapes=[
            pltpu.VMEM((devs, CAP, half, 2 * samples), BF16),
            pltpu.VMEM((devs, HALF, half, 2 * punits), F32),
            pltpu.VMEM((devs, HALF, half, 2 * punits), BF16),
            pltpu.VMEM(head_part.shape, F32),
            pltpu.VMEM((genes * units, samples), F32),
        ]
        + [pltpu.SemaphoreType.DMA((devs,))] * 4
        + [pltpu.SemaphoreType.DMA((8,))],
        compiler_params=pltpu.CompilerParams(
            collective_id=1, has_side_effects=True, vmem_limit_bytes=LIMIT
        ),
        name="return_links",
    )(
        tab,
        deltas.reshape(devs + 1, CAP, half, 2 * samples),
        link_parts.reshape(devs + 1, CAP, half, 2 * punits),
        head_part,
        hidden,
    )

    per = links // steps
    grad_gene, grad_pathway = pl.pallas_call(
        functools.partial(backward_kernel, units),
        out_shape=(shape((units, variants), F32), shape((links, units * punits), F32)),
        grid=(steps,),
        in_specs=[
            smem(),
            pl.BlockSpec((samples, STEP), lambda i: (0, i)),
            pl.BlockSpec((samples, STEP), lambda i: (0, i)),
            vmem(),
            vmem(),
            vmem(),
        ],
        out_specs=(
            pl.BlockSpec((units, STEP), lambda i: (0, i)),
            pl.BlockSpec((per, units * punits), lambda i: (i, 0)),
        ),
        scratch_shapes=[pltpu.VMEM((8 * per, 128), F32)],
        compiler_params=pltpu.CompilerParams(vmem_limit_bytes=LIMIT),
        name="gene_backward",
    )(tab, genotypes, sibling, own, sib, got_parts.reshape(devs * CAP, half, 2 * punits))
    return grad_gene, grad_pathway, grad_head.reshape(-1)


def solution(mesh):
    return jax.shard_map(
        on_device,
        mesh=mesh,
        in_specs=(
            P("batch", "genes"), P(None, "genes"), P("genes"), P(), P(),
            P("genes", None), P("genes"), P("batch"),
        ),
        out_specs=(P(None, "genes"), P("genes", None), P("genes")),
        check_vma=False,
    )
```

time: 909 us -> 199 us (0.22); the launches traced: 899 us -> 198 us
  waiting for transfers between devices: 360 us -> 0 us
  local copies, waits for them, and re-layouts: 359 us -> 1.67 us
  Pallas kernels: 0 us -> 194 us
  matrix products: 83.1 us -> 0 us
  starting transfers between devices: 49.5 us -> 0 us
  other arithmetic: 26.7 us -> 1.29 us
  between operations: 14.8 us -> 0.66 us
    all_to_all x2 -> x0, waiting for transfers between devices: 321 us -> none  [the longest x1 172 us: on_device(): lax.all_to_all(returned.reshape(devices, capacity, path_units, samples),...]
    gather x6 -> x0, local copies, waits for them, and re-layouts: 247 us -> none  [the longest x3 244 us: on_device(): slot_all = jnp.take(pathway_slot, membership.reshape(-1))]
    pallas_call x0 -> x6, Pallas kernels: none -> 194 us  [the longest x1 63.7 us: on_device(): pl.pallas_call(functools.partial(send_kernel, devs), out_shape=(shape((de...]
    dot_general x11 -> x0, matrix products: 83.1 us -> none  [the longest x2 15 us: contract_first(): lax.dot_general(left, right, (((0,), (0,)), ((), ())), preferred_element_...]
    reshape x11 -> x0, local copies, waits for them, and re-layouts: 57.1 us -> none  [the longest x4 27.2 us: on_device(): slot_all = jnp.take(pathway_slot, membership.reshape(-1))]
    all_to_all x2 -> x0, starting transfers between devices: 49.5 us -> none  [the longest x1 28.6 us: on_device(): lax.all_to_all(returned.reshape(devices, capacity, path_units, samples),...]
    unnamed x29 -> x6, local copies, waits for them, and re-layouts: 43.5 us -> 1.67 us
    psum x1 -> x0, waiting for transfers between devices: 38.3 us -> none  [on_device(): lax.psum((grad_rows, grad_links, grad_head), 'batch')]
  transfers between devices with their start and end apart: 3 -> 0, of which waited for: 3 -> 0; matrix products, arithmetic and copies ran while one was open for 3% -> 0% of each run, Pallas kernels for 0% -> 0%
where the time goes in v1:
time: 199 us; the launch traced here: 198 us
  Pallas kernels  194 us (97%)
    pallas_call x1, Pallas kernels, on_device(): pl.pallas_call(functools.partial(send_kernel, devs), out_shape=(shape((de...  63.7 us
    pallas_call x1, Pallas kernels, on_device(): pl.pallas_call(functools.partial(return_kernel, devs, genes, units), out_...  62.4 us
    pallas_call x1, Pallas kernels, on_device(): pl.pallas_call(functools.partial(backward_kernel, units), out_shape=(shap...  22 us
    pallas_call x1, Pallas kernels, on_device(): pl.pallas_call(functools.partial(path_kernel, paths, punits), out_shape=(...  19.7 us
    pallas_call x1, Pallas kernels, on_device(): pl.pallas_call(functools.partial(forward_kernel, genes, units), out_shape...  18.7 us
    pallas_call x1, Pallas kernels, on_device(): pl.pallas_call(functools.partial(index_kernel, devs, genes, paths), out_s...  8.07 us

profile of v1, /device:TPU:1, one launch (start us, length us, event | category | flops | bytes accessed | tf_op | source)
XLA Modules:
  0.0 198.1 jit_solution(11166668298495936242)
XLA Ops:
  0.6 1.3 bitcast_convert_fusion.head_ref
  1.9 8.1 %index.1.tab_ref = s32[40,128]{1,0:T(8,128)} custom-call(s32[2,12288]{1,0:T(2,128)} %bitcast.22, s32[16,128]{1,0:T(8,128)} %bitcast.23, s32[1,192]{1,0:T(1,128)} %bitcast.25), custom_call_target="tpu_custom_call" | custom-call | tf_op jit(solution)/shard_map/index/pallas_call | solution.py:555
  10.0 0.0 copy-start
  10.0 18.7 %gene_forward.1.hid_ref = bf16[192,8,256]{2,1,0:T(8,128)(2,1)} custom-call(s32[40,128]{1,0:T(8,128)} %index.1.tab_ref, bf16[128,49152]{1,0:T(8,128)(2,1)} %own_ref.1, bf16[16,49152]{1,0:T(8,128)(2,1)} %weight_ref.1), custom_call_target="tpu_custom_call" | custom-call | tf_op jit(solution)/shard_map/gene_forward/pallas_call | solution.py:565
  28.7 0.0 copy-done
  28.7 1.1 copy.11
  29.7 63.7 %send_links.1 = (bf16[65,12,8,256]{3,2,1,0:T(8,128)(2,1)}, bf16[65,12,8,128]{3,2,1,0:T(8,128)(2,1)}, bf16[128,49152]{1,0:T(8,128)(2,1)}) custom-call(s32[40,128]{1,0:T(8,128)} %index.1.tab_ref, bf16[192,8,256]{2,1,0:T(8,128)(2,1)} %gene_forward.1.hid_ref, bf16[384,8,128]{2,1,0:T(8,128)(2,1)} %bitcast.18, bf16[128,49152]{1,0:T(8,128)(2,1)} %own_ref.1), custom_call_target="tpu_custom_call" | custom-call | tf_op jit(solution)/shard_map/send_links/pallas_call | solution.py:581
  93.4 19.7 %pathways.1 = (bf16[780,8,256]{2,1,0:T(8,128)(2,1)}, f32[780,8,128]{2,1,0:T(8,128)}, f32[16,128]{1,0:T(8,128)}) custom-call(s32[40,128]{1,0:T(8,128)} %index.1.tab_ref, bf16[780,8,256]{2,1,0:T(8,128)(2,1)} %bitcast.15, bf16[780,8,128]{2,1,0:T(8,128)(2,1)} %bitcast.19, f32[16,128]{1,0:T(8,128)} %bitcast_convert_fusion.head_ref, f32[1,128]{1,0:T(1,128)} %bitcast.26), custom_call_target="tpu_custom_call" | custom-call | tf_op jit(solution)/shard_map/pathways/pallas_call | solution.py:603
  113.1 62.4 %return_links.1 = (bf16[3104,128]{1,0:T(8,128)(2,1)}, bf16[3104,128]{1,0:T(8,128)(2,1)}, bf16[64,12,8,128]{3,2,1,0:T(8,128)(2,1)}, f32[16,128]{1,0:T(8,128)}) custom-call(s32[40,128]{1,0:T(8,128)} %index.1.tab_ref, bf16[65,12,8,256]{3,2,1,0:T(8,128)(2,1)} %bitcast.16, f32[65,12,8,128]{3,2,1,0:T(8,128)} %bitcast.17, f32[16,128]{1,0:T(8,128)} %get-tuple-element.20.gh_ref, ...), custom_call_target="tpu_custom_call" | custom-call | tf_op jit(solution)/shard_map/return_links/pallas_call | solution.py:629
  175.5 0.0 copy-start.1
  175.5 22.0 %gene_backward.1 = (f32[16,49152]{1,0:T(8,128)}, f32[384,1024]{1,0:T(8,128)}) custom-call(s32[40,128]{1,0:T(8,128)} %index.1.tab_ref, bf16[128,49152]{1,0:T(8,128)(2,1)} %own_ref.1, bf16[128,49152]{1,0:T(8,128)(2,1)} %get-tuple-element.15.sib_ref, bf16[3104,128]{1,0:T(8,128)(2,1)} %get-tuple-element.21.pd_own, bf16[3104,128]{1,0:T(8,128)(2,1)} %get-tuple-element.22.pd_sib, ...), custom_call_target="tpu_custom_call" | custom-call | tf_op jit(solution)/shard_map/gene_backward/pallas_call | solution.py:661
  197.5 0.0 copy-done.1
  197.5 0.6 copy.13
Async XLA Ops:
  10.0 18.7 %copy-start = (bf16[384,1024]{1,0:T(8,128)(2,1)S(1)}, bf16[384,1024]{1,0:T(8,128)(2,1)}, u32[]{:S(2)}) copy-start(bf16[384,1024]{1,0:T(8,128)(2,1)} %param.13) | copy-start | bytes 2359300
  175.5 22.0 %copy-start.1 = (f32[16,128]{1,0:T(8,128)S(1)}, f32[16,128]{1,0:T(8,128)}, u32[]{:S(2)}) copy-start(f32[16,128]{1,0:T(8,128)} %get-tuple-element.26) | copy-start | bytes 24580

commit v2 on v1

v2 whole, which is shorter than its diff:
```python
import functools

import jax
import jax.numpy as jnp
from jax import lax
from jax.experimental import pallas as pl
from jax.experimental.pallas import tpu as pltpu
from jax.sharding import PartitionSpec as P

MESH = pl.DeviceIdType.MESH
F32 = jnp.float32
BF16 = jnp.bfloat16
I32 = jnp.int32

CAP = 12
HALF = CAP // 2
COLS = 256
GROUP = 32
MAX_GROUPS = 56
STRIDE = 27

ROW_SEND = 0
ROW_PERM = 12
ROW_SLOT = 26
ROW_RET = 28
ROW_OWNER = 32
ROW_ORDER = 36
ROW_FIRST = 40
ROW_ONE = 42
ROW_TWO = 44
ROW_PART = 46
TAB_ROWS = 56
CHUNK = 4096
PARTS = 3


def iota(shape, dim):
    return lax.broadcasted_iota(I32, shape, dim)


def one(mask):
    return jnp.where(mask, 1.0, 0.0).astype(BF16)


def mm(left, right):
    return jnp.dot(left, right, preferred_element_type=F32)


def mm_tn(left, right):
    return lax.dot_general(left, right, (((0,), (0,)), ((), ())), preferred_element_type=F32)


def mm_nt(left, right):
    return lax.dot_general(left, right, (((1,), (1,)), ((), ())), preferred_element_type=F32)


def to_col(row, n):
    eye = iota((n, n), 0) == iota((n, n), 1)
    return jnp.sum(jnp.where(eye, jnp.broadcast_to(row, (n, n)), 0.0), axis=1, keepdims=True)


def to_row(col, n):
    eye = iota((n, n), 0) == iota((n, n), 1)
    return jnp.sum(jnp.where(eye, jnp.broadcast_to(col, (n, n)), 0.0), axis=0, keepdims=True)


def put(tab_ref, row, values):
    width = values.shape[1]
    tab_ref[row : row + 1, :] = values[:, :128]
    tab_ref[row + 1 : row + 2, : width - 128] = values[:, 128:]


def index_kernel(
    devs, genes, paths, mem_ref, slot_ref, len_ref, link_ref, tab_ref, rows_ref,
    s_ref, own_ref, tile_ref,
):
    me = lax.axis_index("genes")
    per = genes
    table = slot_ref[...]
    halves = jnp.concatenate([table >> 5, table & 31], axis=0).astype(F32).astype(BF16)
    rows = table.shape[0]
    pair = 2 * per

    for m in range(2):
        def look(j, _, m=m):
            q = mem_ref[m : m + 1, pl.ds(pl.multiple_of(j * pair, 128), pair)]
            lane = q & 127
            which = q >> 7
            hot = one(jnp.broadcast_to(lane, (128, pair)) == iota((128, pair), 0))
            vals = mm(halves, hot)
            pick = jnp.broadcast_to(which, (rows, pair)) == iota((rows, pair), 0)
            owner = jnp.sum(jnp.where(pick, vals[:rows], 0.0), axis=0, keepdims=True)
            local = jnp.sum(jnp.where(pick, vals[rows:], 0.0), axis=0, keepdims=True)
            slot = owner * 32.0 + local
            s_ref[pl.ds(m * devs + 2 * j, 1), :] = slot[:, :per]
            s_ref[pl.ds(m * devs + 2 * j + 1, 1), :] = slot[:, per:]
            return 0

        lax.fori_loop(0, devs // 2, look, 0, unroll=4)

    tab_ref[...] = jnp.zeros((TAB_ROWS, 128), I32)
    slots = s_ref[...].astype(I32)
    mine = (slots >> 5) == me
    local = (slots & 31).astype(F32)
    upper = one(iota((per, per), 0) < iota((per, per), 1))
    before = mm(one(mine), upper)
    count = jnp.sum(jnp.where(mine, 1.0, 0.0), axis=1, keepdims=True)
    lead = jnp.concatenate([jnp.zeros((devs, 1), F32), count[:devs]], axis=0)
    rank = before + lead
    lower = one(iota((devs, devs), 1) < iota((devs, devs), 0))
    lane64 = iota((devs, 128), 1)
    carry = jnp.zeros((1, 128), F32)
    places, cells = [], []
    for r in range(CAP):
        hit = mine & (rank == float(r))
        got = jnp.sum(jnp.where(hit, local + 1.0, 0.0), axis=1, keepdims=True)
        got = got[:devs] + got[devs:]
        cell = jnp.where(got == 0.0, float(paths), got - 1.0).astype(I32)
        hot = jnp.broadcast_to(cell, (devs, 128)) == lane64
        within = mm(lower, one(hot)) + carry
        carry = carry + jnp.sum(jnp.where(hot, 1.0, 0.0), axis=0, keepdims=True)
        places.append(jnp.sum(jnp.where(hot, within, 0.0), axis=1, keepdims=True))
        cells.append(hot)
    lane1 = iota((1, 128), 1)
    groups = jnp.where(lane1 < paths, ((carry.astype(I32) + (GROUP - 1)) // GROUP).astype(F32), 0.0)
    strict = one(iota((128, 128), 0) < iota((128, 128), 1))
    start = mm(jnp.broadcast_to(groups.astype(BF16), (8, 128)), strict)[:1]
    end_col = to_col(start + groups, 128)
    ends = jnp.where(
        (jnp.broadcast_to(end_col, (128, 128)) <= iota((128, 128), 1).astype(F32))
        & (iota((128, 128), 0) < paths),
        1.0,
        0.0,
    )
    tab_ref[ROW_SLOT : ROW_SLOT + 1, :] = jnp.sum(ends, axis=0, keepdims=True).astype(I32)
    total = jnp.sum(groups, axis=1, keepdims=True)
    tab_ref[ROW_SLOT + 1 : ROW_SLOT + 2, :] = jnp.broadcast_to(total, (1, 128)).astype(I32)
    src_sum = jnp.zeros((16, 128), F32)
    rank_sum = jnp.zeros((16, 128), F32)
    seen = jnp.zeros((16, 128), F32)
    source = iota((devs, 128), 0).astype(F32).astype(BF16)
    for r in range(CAP):
        first = jnp.sum(
            jnp.where(cells[r], jnp.broadcast_to(start, (devs, 128)), 0.0), axis=1, keepdims=True
        )
        real = jnp.sum(jnp.where(cells[r] & (lane64 < paths), 1.0, 0.0), axis=1, keepdims=True)
        pos = (first * float(GROUP) + places[r]).astype(I32)
        pos = jnp.where(real > 0.0, pos, 1 << 20)
        high = one(jnp.broadcast_to(pos >> 7, (devs, 16)) == iota((devs, 16), 1))
        low = jnp.broadcast_to(pos & 127, (devs, 128)) == lane64
        src_sum = src_sum + mm_tn(high, jnp.where(low, source, jnp.zeros((), BF16)))
        found = mm_tn(high, one(low))
        rank_sum = rank_sum + found * float(r)
        seen = seen + found
    perm = jnp.where(seen > 0.0, src_sum * float(CAP) + rank_sum, float(devs * CAP))
    tab_ref[ROW_PERM : ROW_PERM + 14, :] = perm.astype(I32)[:14]

    own_ref[0:1, :] = s_ref[pl.ds(me, 1), :]
    own_ref[1:2, :] = s_ref[pl.ds(devs + me, 1), :]
    lower_g = one(iota((per, per), 1) < iota((per, per), 0))
    lane_g = iota((per, 128), 1)
    gene_col = iota((per, 128), 0).astype(F32).astype(BF16)
    carry = jnp.zeros((1, 128), F32)
    send = jnp.zeros((16, 128), F32)
    owner_rows = [own_ref[m : m + 1, :].astype(I32) >> 5 for m in range(2)]
    for m in range(2):
        owner = (to_col(own_ref[m : m + 1, :], per).astype(I32)) >> 5
        hot = jnp.broadcast_to(owner, (per, 128)) == lane_g
        within = mm(lower_g, one(hot)) + carry
        carry = carry + jnp.sum(jnp.where(hot, 1.0, 0.0), axis=0, keepdims=True)
        order = jnp.sum(jnp.where(hot, within, 0.0), axis=1, keepdims=True)
        cell = one(jnp.broadcast_to(order, (per, 16)) == iota((per, 16), 1).astype(F32))
        send = send + 2.0 * mm_tn(cell, jnp.where(hot, gene_col, jnp.zeros((), BF16)))
        if m:
            send = send + mm_tn(cell, one(hot))
        owner_row = owner_rows[m]
        order_row = to_row(order, per).astype(I32)
        put(tab_ref, ROW_RET + 2 * m, owner_row * CAP + order_row)
        put(tab_ref, ROW_OWNER + 2 * m, owner_row)
        put(tab_ref, ROW_ORDER + 2 * m, order_row)
    tab_ref[ROW_SEND : ROW_SEND + CAP, :] = send.astype(I32)[:CAP]

    lens = len_ref[...].astype(F32) - 128.0
    starts = mm(jnp.broadcast_to(lens.astype(BF16), (8, per)), upper)[:1]
    starts = starts + 128.0 * iota((1, per), 1).astype(F32)
    start_col = jnp.broadcast_to(to_col(starts, per), (per, 256))
    begin = (iota((per, 256), 1) * COLS).astype(F32)
    inside = jnp.where(start_col <= begin, 1.0, 0.0)
    put(tab_ref, ROW_FIRST, (jnp.sum(inside, axis=0, keepdims=True) - 1.0).astype(I32))
    end = float(per * COLS)
    next_one = jnp.min(jnp.where(start_col > begin, start_col, end), axis=0, keepdims=True)
    next_two = jnp.min(
        jnp.where(start_col > jnp.broadcast_to(next_one, (per, 256)), start_col, end),
        axis=0, keepdims=True,
    )
    put(tab_ref, ROW_ONE, (next_one - begin[:1]).astype(I32))
    put(tab_ref, ROW_TWO, (next_two - begin[:1]).astype(I32))
    start_col = start_col[:, :per]
    starts_i = starts.astype(I32)
    last = (starts_i + len_ref[...] - 1) >> 8
    gene_row = iota((1, per), 1)
    for j in range(PARTS):
        block = (starts_i >> 8) + j
        edge = jnp.broadcast_to((block * COLS).astype(F32), (per, per))
        under = jnp.where(start_col <= edge, 1.0, 0.0)
        lead_gene = jnp.sum(under, axis=0, keepdims=True).astype(I32) - 1
        row = block * PARTS + (gene_row - lead_gene)
        put(tab_ref, ROW_PART + 2 * j, jnp.where(block <= last, row, per * PARTS))

    def relayout(e, _):
        at = pl.multiple_of(16 * e, 16)
        rows = link_ref[pl.ds(at, 16), :].astype(F32)
        for n in range(2):
            for t in range(8):
                tile_ref[pl.ds(64 * n + t, 8, stride=8), :] = rows[
                    8 * n : 8 * n + 8, 128 * t : 128 * t + 128
                ]
        for n in range(16):
            rows_ref[at + n] = tile_ref[8 * n : 8 * n + 8, :].astype(BF16)
        return 0

    lax.fori_loop(0, link_ref.shape[0] // 16, relayout, 0)


def look_up(tab_ref, row, index):
    return tab_ref[row + (index >> 7), index & 127]


def window_of(tab_ref, block):
    return tuple(look_up(tab_ref, row, block) for row in (ROW_FIRST, ROW_ONE, ROW_TWO))


def partner(me, k):
    off = lax.rem(k * STRIDE, 64)
    x = lax.rem(me // 16 + off // 16, 4)
    z = lax.rem((me // 4) % 4 + (off // 4) % 4, 4)
    y = lax.rem(me % 4 + off % 4, 4)
    return x * 16 + z * 4 + y


def greet(devs, me, core):
    barrier = pltpu.get_barrier_semaphore()

    def hello(k, _):
        pl.semaphore_signal(
            barrier, inc=1, device_id=(partner(me, k), core), device_id_type=MESH
        )
        return 0

    lax.fori_loop(1, devs, hello, 0)
    pl.semaphore_signal(barrier, inc=1, device_id=(me, 1 - core), device_id_type=MESH)
    pl.semaphore_wait(barrier, devs)


def load_chunks(src_ref, dst_ref, sem):
    return [
        pltpu.make_async_copy(
            src_ref.at[:, pl.ds(c * CHUNK, CHUNK)], dst_ref.at[:, pl.ds(c * CHUNK, CHUNK)], sem.at[c]
        )
        for c in range(src_ref.shape[1] // CHUNK)
    ]


def send_kernel(
    devs, genes, units, tab_ref, link_ref, geno_ref, weight_ref, hid_ref, h_ref, w_ref,
    g_ref, gw_ref, part_ref, pre_ref, hs_ref, ws_ref, geno_sem, weight_sem, hsend, hrecv, wsend, wrecv,
    pair_sem,
):
    me = lax.axis_index("genes")
    core = lax.axis_index("batch")
    low = core * HALF
    loads = load_chunks(geno_ref, g_ref, geno_sem)
    weights = load_chunks(weight_ref, gw_ref, weight_sem)
    for weight, load in zip(weights, loads):
        weight.start()
        load.start()
    greet(devs, me, core)

    def w_copy(k):
        to = partner(me, k)
        return pltpu.make_async_remote_copy(
            src_ref=ws_ref.at[to], dst_ref=w_ref.at[me, pl.ds(low, HALF)],
            send_sem=wsend, recv_sem=wrecv,
            device_id=(to, core), device_id_type=MESH,
        )

    def h_copy(k):
        to = partner(me, k)
        return pltpu.make_async_remote_copy(
            src_ref=hs_ref.at[to], dst_ref=h_ref.at[me],
            send_sem=hsend, recv_sem=hrecv,
            device_id=(to, core), device_id_type=MESH,
        )

    def w_step(k, _):
        to = partner(me, k)
        for r in range(HALF):
            ws_ref[to, r] = link_ref[tab_ref[low + r, to]]
        w_copy(k).start()
        return 0

    lax.fori_loop(1, devs, w_step, 0)

    pos = iota((units, COLS), 1)
    part_ref[genes * PARTS] = jnp.zeros((units, 128), F32)
    per_chunk = CHUNK // COLS
    for c, load in enumerate(loads):
        weights[c].wait()
        load.wait()

        def block(i, _, c=c):
            for k in range(4):
                b = c * per_chunk + i * 4 + k
                _, one_end, two_end = window_of(tab_ref, b)
                cols = pl.ds(pl.multiple_of(b * COLS, COLS), COLS)
                weight = gw_ref[:, cols].astype(F32)
                not_one = pos >= one_end
                not_two = pos >= two_end
                zero = jnp.zeros_like(weight)
                basis = jnp.concatenate(
                    [
                        jnp.where(not_one, zero, weight),
                        jnp.where(not_one & jnp.logical_not(not_two), weight, zero),
                        jnp.where(not_two, weight, zero),
                    ],
                    axis=0,
                ).astype(BF16)
                got = mm_nt(basis, g_ref[:, cols])
                for w in range(PARTS):
                    part_ref[b * PARTS + w] = got[w * units : (w + 1) * units]
            return 0

        lax.fori_loop(0, per_chunk // 4, block, 0)

    def finish(i, _):
        for k in range(8):
            g = i * 8 + k
            total = part_ref[look_up(tab_ref, ROW_PART, g)]
            for j in range(1, PARTS):
                total = total + part_ref[look_up(tab_ref, ROW_PART + 2 * j, g)]
            pre_ref[pl.ds(k * units, units), :] = jnp.tanh(total)
        for k in range(8):
            even = pre_ref[pl.ds(k * units, units // 2, stride=2), :]
            odd = pre_ref[pl.ds(k * units + 1, units // 2, stride=2), :]
            hid_ref[i * 8 + k] = jnp.concatenate([even, odd], axis=1).astype(BF16)
        return 0

    lax.fori_loop(0, genes // 8, finish, 0)

    def h_step(k, _):
        to = partner(me, k)
        for r in range(CAP):
            hs_ref[to, r] = hid_ref[tab_ref[r, to] >> 1]
        h_copy(k).start()
        return 0

    lax.fori_loop(1, devs, h_step, 0)
    for r in range(CAP):
        h_ref[me, r] = hid_ref[tab_ref[r, me] >> 1]
    for r in range(HALF):
        w_ref[me, low + r] = link_ref[tab_ref[low + r, me]]
    h_ref[devs] = jnp.zeros(h_ref.shape[1:], BF16)
    w_ref[devs] = jnp.zeros(w_ref.shape[1:], BF16)

    others = pl.ds(0, devs - 1)
    pltpu.make_async_remote_copy(
        src_ref=ws_ref.at[others], dst_ref=w_ref.at[others, pl.ds(low, HALF)],
        send_sem=wsend, recv_sem=wrecv, device_id=(me, 1 - core), device_id_type=MESH,
    ).wait()
    part = w_ref.at[pl.ds(0, devs), pl.ds(low, HALF)]
    share = pltpu.make_async_remote_copy(
        src_ref=part, dst_ref=part, send_sem=pair_sem.at[0], recv_sem=pair_sem.at[1],
        device_id=(me, 1 - core), device_id_type=MESH,
    )
    share.start()

    pltpu.make_async_remote_copy(
        src_ref=hs_ref.at[others], dst_ref=h_ref.at[others],
        send_sem=hsend, recv_sem=hrecv, device_id=(me, 1 - core), device_id_type=MESH,
    ).wait()
    share.wait()


def path_kernel(
    paths, punits, tab_ref, h_ref, w_ref, head_ref, cot_ref, hd_ref, gp_ref, gh_ref,
    hs_ref, ws_ref, sum_ref, delta_ref, heads,
):
    rows = (tab_ref[ROW_SLOT + 1, 0] + 3) // 4
    sum_ref[...] = jnp.zeros_like(sum_ref)

    def up(i, _):
        for q in range(4):
            for j in range(GROUP):
                p = tab_ref[ROW_PERM + i, q * GROUP + j]
                hs_ref[4 * i + q, 8 * j : 8 * j + 8, :] = h_ref[p]
                ws_ref[4 * i + q, 8 * j : 8 * j + 8, :] = w_ref[p]
            slot = tab_ref[ROW_SLOT, 4 * i + q]
            out = mm_tn(ws_ref[4 * i + q], hs_ref[4 * i + q])
            sum_ref[slot] = sum_ref[slot] + out[:punits, :128] + out[punits:, 128:]
        return 0

    lax.fori_loop(0, rows, up, 0)

    cot = cot_ref[...]
    heads[...] = head_ref[...].astype(F32)
    lane = iota((punits, 128), 1)
    sub = iota((punits, 128), 0)

    def middle(i, _):
        row = jnp.zeros((1, 128), F32)
        head_row = heads[pl.ds(i, 1), :]
        for half in range(2):
            s = 2 * i + half
            active = jnp.tanh(sum_ref[s])
            diag = lane == sub + punits * half
            head = jnp.sum(
                jnp.where(diag, jnp.broadcast_to(head_row, (punits, 128)), 0.0),
                axis=1, keepdims=True,
            )
            grad = jnp.sum(active * cot, axis=1, keepdims=True)
            row = row + jnp.sum(
                jnp.where(diag, jnp.broadcast_to(grad, (punits, 128)), 0.0), axis=0, keepdims=True
            )
            delta = (cot * head * (1.0 - active * active)).astype(BF16)
            none = jnp.zeros_like(delta)
            delta_ref[s] = jnp.concatenate(
                [
                    jnp.concatenate([delta, none], axis=1),
                    jnp.concatenate([none, delta], axis=1),
                ],
                axis=0,
            )
        gh_ref[pl.ds(i, 1), :] = row
        return 0

    lax.fori_loop(0, paths // 2, middle, 0)
    delta_ref[paths] = jnp.zeros(delta_ref.shape[1:], BF16)

    def down(i, _):
        for q in range(4):
            block = delta_ref[tab_ref[ROW_SLOT, 4 * i + q]]
            hd = mm(ws_ref[4 * i + q], block).astype(BF16)
            gp = mm_nt(hs_ref[4 * i + q], block)
            for j in range(GROUP):
                p = tab_ref[ROW_PERM + i, q * GROUP + j]
                hd_ref[p] = hd[8 * j : 8 * j + 8]
                gp_ref[p] = gp[8 * j : 8 * j + 8]
        return 0

    lax.fori_loop(0, rows, down, 0)


def return_kernel(
    devs, genes, units, tab_ref, hd_ref, gp_ref, gh_ref, hid_ref, geno_ref,
    out_ref, path_ref, head_ref,
    g_ref, back_ref, part_ref, gs_ref, link_ref, ghs_ref, pd_ref, own_ref, sib_ref, grad_ref, rows_ref,
    geno_sem, out_sem, hsend, hrecv, gsend, grecv, pair_sem,
):
    me = lax.axis_index("genes")
    core = lax.axis_index("batch")
    low = core * HALF
    other = (1 - core) * HALF
    samples = geno_ref.shape[0]
    span = geno_ref.shape[1] // 2
    here = pl.multiple_of(core * span, span)
    there = pl.multiple_of((1 - core) * span, span)
    load = pltpu.make_async_copy(
        geno_ref.at[:, pl.ds(here, span)], g_ref.at[pl.ds(0, samples)], geno_sem
    )
    load.start()
    greet(devs, me, core)

    def pair(src, dst, n):
        return pltpu.make_async_remote_copy(
            src_ref=src, dst_ref=dst, send_sem=pair_sem.at[2 * n], recv_sem=pair_sem.at[2 * n + 1],
            device_id=(me, 1 - core), device_id_type=MESH,
        )

    def h_copy(k):
        to = partner(me, k)
        return pltpu.make_async_remote_copy(
            src_ref=hd_ref.at[pl.ds(to * CAP, CAP)], dst_ref=back_ref.at[pl.ds(me * CAP, CAP)],
            send_sem=hsend, recv_sem=hrecv,
            device_id=(to, core), device_id_type=MESH,
        )

    def g_copy(k):
        to = partner(me, k)
        return pltpu.make_async_remote_copy(
            src_ref=gs_ref.at[to], dst_ref=link_ref.at[me, pl.ds(low, HALF)],
            send_sem=gsend, recv_sem=grecv,
            device_id=(to, core), device_id_type=MESH,
        )

    def h_step(k, _):
        h_copy(k).start()
        return 0

    lax.fori_loop(1, devs, h_step, 0)
    parts = pair(gp_ref.at[pl.ds(0, devs), pl.ds(other, HALF)], part_ref, 0)
    parts.start()
    heads = pair(gh_ref, ghs_ref, 1)
    heads.start()
    geno = pair(geno_ref.at[:, pl.ds(there, span)], g_ref.at[pl.ds(samples, samples)], 2)
    geno.start()
    back_ref[pl.ds(me * CAP, CAP)] = hd_ref[pl.ds(me * CAP, CAP)]
    parts.wait()

    def g_step(k, _):
        to = partner(me, k)
        gs_ref[to] = (gp_ref[to, pl.ds(low, HALF)] + part_ref[to]).astype(BF16)
        g_copy(k).start()
        return 0

    lax.fori_loop(1, devs, g_step, 0)
    link_ref[me, pl.ds(low, HALF)] = (gp_ref[me, pl.ds(low, HALF)] + part_ref[me]).astype(BF16)
    heads.wait()
    head_ref[...] = gh_ref[...] + ghs_ref[...]
    for n in range(genes, own_ref.shape[0]):
        own_ref[n] = jnp.zeros((units, 128), BF16)
        sib_ref[n] = jnp.zeros((units, 128), BF16)

    others = pl.ds(0, devs - 1)
    pltpu.make_async_remote_copy(
        src_ref=hd_ref.at[pl.ds(0, (devs - 1) * CAP)],
        dst_ref=back_ref.at[pl.ds(0, (devs - 1) * CAP)],
        send_sem=hsend, recv_sem=hrecv, device_id=(me, 1 - core), device_id_type=MESH,
    ).wait()

    def gene(i, _):
        for k in range(4):
            g = 4 * i + k
            a = look_up(tab_ref, ROW_RET, g)
            b = look_up(tab_ref, ROW_RET + 2, g)
            both = back_ref[a].astype(F32) + back_ref[b].astype(F32)
            hid = hid_ref[g].astype(F32)
            value = both * (1.0 - hid * hid)
            pd_ref[pl.ds(k * units, units // 2, stride=2), :] = value[:, :128]
            pd_ref[pl.ds(k * units + 1, units // 2, stride=2), :] = value[:, 128:]
        for k in range(4):
            own_ref[4 * i + k] = pd_ref[pl.ds(k * units, units), :].astype(BF16)
        return 0

    quarter = genes // 4
    deltas = []
    for n in range(4):
        lax.fori_loop(n * quarter // 4, (n + 1) * quarter // 4, gene, 0)
        rows = pl.ds(n * quarter, quarter)
        delta = pair(own_ref.at[rows], sib_ref.at[rows], 4 + n)
        delta.start()
        deltas.append(delta)
    load.wait()
    geno.wait()
    for delta in deltas:
        delta.wait()

    pos = iota((units, COLS), 1)
    per_chunk = CHUNK // COLS
    stores = []
    first_block = core * (span // COLS)
    for c in range(span // CHUNK):
        def block(i, _, c=c):
            for k in range(4):
                b = c * per_chunk + i * 4 + k
                first, one_end, two_end = window_of(tab_ref, first_block + b)
                left = jnp.concatenate(
                    [
                        jnp.concatenate([ref[first + w] for w in range(PARTS)], axis=0)
                        for ref in (own_ref, sib_ref)
                    ],
                    axis=1,
                )
                cols = pl.ds(pl.multiple_of(b * COLS, COLS), COLS)
                full = mm(left, g_ref[:, cols])
                grad_ref[:, cols] = jnp.where(
                    pos >= two_end,
                    full[2 * units :],
                    jnp.where(pos >= one_end, full[units : 2 * units], full[:units]),
                )
            return 0

        lax.fori_loop(0, per_chunk // 4, block, 0)
        cols = pl.ds(pl.multiple_of(here + c * CHUNK, CHUNK), CHUNK)
        piece = grad_ref.at[:, pl.ds(c * CHUNK, CHUNK)]
        store = pltpu.make_async_copy(piece, out_ref.at[:, cols], out_sem.at[c])
        store.start()
        stores.append(store)
        store = pair(piece, out_ref.at[:, cols], 8 + c)
        store.start()
        stores.append(store)

    pltpu.make_async_remote_copy(
        src_ref=gs_ref.at[others], dst_ref=link_ref.at[others, pl.ds(low, HALF)],
        send_sem=gsend, recv_sem=grecv, device_id=(me, 1 - core), device_id_type=MESH,
    ).wait()
    part = link_ref.at[pl.ds(0, devs), pl.ds(low, HALF)]
    share = pair(part, part, 3)
    share.start()
    share.wait()

    def link_group(e, _):
        for j in range(8):
            g = e * 4 + j // 2
            owner = look_up(tab_ref, ROW_OWNER + 2 * (j % 2), g)
            order = look_up(tab_ref, ROW_ORDER + 2 * (j % 2), g)
            rows_ref[8 * j : 8 * j + 8, :] = link_ref[owner, order].astype(F32)
        for t in range(8):
            path_ref[pl.ds(pl.multiple_of(8 * e, 8), 8), 128 * t : 128 * t + 128] = rows_ref[
                pl.ds(t, 8, stride=8), :
            ]
        return 0

    lax.fori_loop(0, path_ref.shape[0] // 8, link_group, 0)
    for store in stores:
        store.wait()


def vmem():
    return pl.BlockSpec(memory_space=pltpu.VMEM)


def smem():
    return pl.BlockSpec(memory_space=pltpu.SMEM)


def hbm():
    return pl.BlockSpec(memory_space=pl.ANY)


LIMIT = 60 * 1024 * 1024


def on_device(
    genotypes, gene_weight, gene_lengths, membership, pathway_slot, pathway_weight,
    head_weight, cotangent,
):
    devs = lax.axis_size("genes")
    genes = gene_lengths.shape[0]
    links = pathway_weight.shape[0]
    units = gene_weight.shape[0]
    samples, variants = genotypes.shape
    punits = pathway_weight.shape[1] // units
    paths = head_weight.shape[0] // punits
    half = units // 2
    shape = jax.ShapeDtypeStruct

    tab, link_rows = pl.pallas_call(
        functools.partial(index_kernel, devs, genes, paths),
        out_shape=(
            shape((TAB_ROWS, 128), I32),
            shape((links, half, 2 * punits), BF16),
        ),
        in_specs=[vmem()] * 4,
        out_specs=(vmem(),) * 2,
        scratch_shapes=[
            pltpu.VMEM((2 * devs, genes), F32),
            pltpu.VMEM((2, genes), F32),
            pltpu.VMEM((128, 128), F32),
        ],
        compiler_params=pltpu.CompilerParams(vmem_limit_bytes=LIMIT),
        name="index",
    )(membership.T, pathway_slot.reshape(-1, 128), gene_lengths.reshape(1, -1), pathway_weight)

    pieces = variants // CHUNK
    hidden, got_hidden, got_links = pl.pallas_call(
        functools.partial(send_kernel, devs, genes, units),
        out_shape=(
            shape((genes, half, 2 * samples), BF16),
            shape((devs + 1, CAP, half, 2 * samples), BF16),
            shape((devs + 1, CAP, half, 2 * punits), BF16),
        ),
        in_specs=[smem(), vmem(), hbm(), hbm()],
        out_specs=(vmem(),) * 3,
        scratch_shapes=[
            pltpu.VMEM((samples, variants), BF16),
            pltpu.VMEM((units, variants), BF16),
            pltpu.VMEM((genes * PARTS + 1, units, samples), F32),
            pltpu.VMEM((8 * units, samples), F32),
            pltpu.VMEM((devs, CAP, half, 2 * samples), BF16),
            pltpu.VMEM((devs, HALF, half, 2 * punits), BF16),
        ]
        + [pltpu.SemaphoreType.DMA((pieces,))] * 2
        + [pltpu.SemaphoreType.DMA(())] * 4
        + [pltpu.SemaphoreType.DMA((2,))],
        compiler_params=pltpu.CompilerParams(
            collective_id=0, has_side_effects=True, vmem_limit_bytes=LIMIT
        ),
        name="send_links",
    )(tab, link_rows, genotypes, gene_weight)

    rows = (devs + 1) * CAP
    deltas, link_parts, head_part = pl.pallas_call(
        functools.partial(path_kernel, paths, punits),
        out_shape=(
            shape((rows, half, 2 * samples), BF16),
            shape((rows, half, 2 * punits), F32),
            shape((paths * punits // 128, 128), F32),
        ),
        in_specs=[smem()] + [vmem()] * 4,
        out_specs=(vmem(),) * 3,
        scratch_shapes=[
            pltpu.VMEM((MAX_GROUPS, 8 * GROUP, 2 * samples), BF16),
            pltpu.VMEM((MAX_GROUPS, 8 * GROUP, 2 * punits), BF16),
            pltpu.VMEM((paths + 1, punits, samples), F32),
            pltpu.VMEM((paths + 1, 2 * punits, 2 * samples), BF16),
            pltpu.VMEM((paths * punits // 128, 128), F32),
        ],
        compiler_params=pltpu.CompilerParams(vmem_limit_bytes=LIMIT),
        name="pathways",
    )(
        tab,
        got_hidden.reshape(rows, half, 2 * samples),
        got_links.reshape(rows, half, 2 * punits),
        head_weight.reshape(-1, 128),
        cotangent.reshape(1, -1),
    )

    grad_gene, grad_pathway, grad_head = pl.pallas_call(
        functools.partial(return_kernel, devs, genes, units),
        out_shape=(
            shape((units, variants), F32),
            shape((links, units * punits), F32),
            shape(head_part.shape, F32),
        ),
        in_specs=[smem()] + [vmem()] * 4 + [hbm()],
        out_specs=(hbm(), vmem(), vmem()),
        scratch_shapes=[
            pltpu.VMEM((2 * samples, variants // 2), BF16),
            pltpu.VMEM((devs * CAP, half, 2 * samples), BF16),
            pltpu.VMEM((devs, HALF, half, 2 * punits), F32),
            pltpu.VMEM((devs, HALF, half, 2 * punits), BF16),
            pltpu.VMEM((devs, CAP, half, 2 * punits), BF16),
            pltpu.VMEM(head_part.shape, F32),
            pltpu.VMEM((4 * units, samples), F32),
            pltpu.VMEM((genes + 2, units, samples), BF16),
            pltpu.VMEM((genes + 2, units, samples), BF16),
            pltpu.VMEM((units, variants // 2), F32),
            pltpu.VMEM((8 * half, 2 * punits), F32),
        ]
        + [pltpu.SemaphoreType.DMA(()), pltpu.SemaphoreType.DMA((pieces // 2,))]
        + [pltpu.SemaphoreType.DMA(())] * 4
        + [pltpu.SemaphoreType.DMA((16 + pieces,))],
        compiler_params=pltpu.CompilerParams(
            collective_id=1, has_side_effects=True, vmem_limit_bytes=LIMIT
        ),
        name="return_links",
    )(
        tab,
        deltas,
        link_parts.reshape(devs + 1, CAP, half, 2 * punits),
        head_part,
        hidden,
        genotypes,
    )
    return grad_gene, grad_pathway, grad_head.reshape(-1)


def solution(mesh):
    return jax.shard_map(
        on_device,
        mesh=mesh,
        in_specs=(
            P("batch", "genes"), P(None, "genes"), P("genes"), P(), P(),
            P("genes", None), P("genes"), P("batch"),
        ),
        out_specs=(P(None, "genes"), P("genes", None), P("genes")),
        check_vma=False,
    )
```

time: 199 us -> 161 us (0.81)
  Pallas kernels: 194 us -> 155 us
  local copies, waits for them, and re-layouts: 1.67 us -> 5.62 us
    pallas_call x3 -> x1, Pallas kernels: 104 us -> 65.9 us  [on_device(): pl.pallas_call(functools.partial(send_kernel, devs, genes, units), out_sh...]
    pallas_call x1, Pallas kernels: 19.7 us -> 14.7 us  [on_device(): pl.pallas_call(functools.partial(path_kernel, paths, punits), out_shape=(...]
    unnamed x6 -> x7, local copies, waits for them, and re-layouts: 1.67 us -> 5.62 us
    pallas_call x1, Pallas kernels: 62.4 us -> 65.3 us  [on_device(): pl.pallas_call(functools.partial(return_kernel, devs, genes, units), out_...]
where the time goes in v2:
time: 161 us
  Pallas kernels  155 us (96%)
  local copies, waits for them, and re-layouts  5.62 us (3%)
    pallas_call x1, Pallas kernels, on_device(): pl.pallas_call(functools.partial(send_kernel, devs, genes, units), out_sh...  65.9 us
    pallas_call x1, Pallas kernels, on_device(): pl.pallas_call(functools.partial(return_kernel, devs, genes, units), out_...  65.3 us
    pallas_call x1, Pallas kernels, on_device(): pl.pallas_call(functools.partial(path_kernel, paths, punits), out_shape=(...  14.7 us
    pallas_call x1, Pallas kernels, on_device(): pl.pallas_call(functools.partial(index_kernel, devs, genes, paths), out_s...  9.16 us
    unnamed x7, local copies, waits for them, and re-layouts  5.62 us

profile of v2, /device:TPU:1, one launch (start us, length us, event | category | flops | bytes accessed | tf_op | source)
XLA Modules:
  0.0 161.3 jit_solution(521372947750952346)
XLA Ops:
  0.6 9.2 %index.1 = (s32[56,128]{1,0:T(8,128)}, bf16[384,8,128]{2,1,0:T(8,128)(2,1)}) custom-call(s32[2,12288]{1,0:T(2,128)} %bitcast.12, s32[16,128]{1,0:T(8,128)} %bitcast.13, s32[1,192]{1,0:T(1,128)} %bitcast.16, bf16[384,1024]{1,0:T(8,128)(2,1)} %link_ref.1), custom_call_target="tpu_custom_call" | custom-call | tf_op jit(solution)/shard_map/index/pallas_call | solution.py:647
  9.8 65.9 %send_links.1 = (bf16[192,8,256]{2,1,0:T(8,128)(2,1)}, bf16[65,12,8,256]{3,2,1,0:T(8,128)(2,1)}, bf16[65,12,8,128]{3,2,1,0:T(8,128)(2,1)}) custom-call(s32[56,128]{1,0:T(8,128)} %get-tuple-element.14.tab_ref, bf16[384,8,128]{2,1,0:T(8,128)(2,1)} %get-tuple-element.15.link_ref, bf16[128,49152]{1,0:T(8,128)(2,1)} %geno_ref.3, bf16[16,49152]{1,0:T(8,128)(2,1)} %weight_ref.1), custom_call_target="tpu_custom_call" | custom-call | tf_op jit(solution)/shard_map/send_links/pallas_call | solution.py:665
  75.7 14.7 %pathways.1 = (bf16[780,8,256]{2,1,0:T(8,128)(2,1)}, f32[780,8,128]{2,1,0:T(8,128)}, f32[16,128]{1,0:T(8,128)}) custom-call(s32[56,128]{1,0:T(8,128)} %get-tuple-element.14.tab_ref, bf16[780,8,256]{2,1,0:T(8,128)(2,1)} %bitcast.10, bf16[780,8,128]{2,1,0:T(8,128)(2,1)} %bitcast.11, bf16[16,128]{1,0:T(8,128)(2,1)} %bitcast.15, f32[1,128]{1,0:T(1,128)} %bitcast.17), custom_call_target="tpu_custom_call" | custom-call | tf_op jit(solution)/shard_map/pathways/pallas_call | solution.py:692
  90.4 65.3 %return_links.1 = (f32[16,49152]{1,0:T(8,128)}, f32[384,1024]{1,0:T(8,128)}, f32[16,128]{1,0:T(8,128)}) custom-call(s32[56,128]{1,0:T(8,128)} %get-tuple-element.14.tab_ref, bf16[780,8,256]{2,1,0:T(8,128)(2,1)} %get-tuple-element.18.hd_ref, f32[65,12,8,128]{3,2,1,0:T(8,128)} %bitcast.9, f32[16,128]{1,0:T(8,128)} %get-tuple-element.20.gh_ref, ...), custom_call_target="tpu_custom_call" | custom-call | tf_op jit(solution)/shard_map/return_links/pallas_call | solution.py:718
  155.7 0.0 copy-start
  155.7 0.0 copy-start.1
  155.7 3.9 %copy.14 = f32[16,49152]{1,0:T(8,128)} copy(f32[16,49152]{1,0:T(8,128)} %get-tuple-element.28) | data formatting | bytes 6291456
  159.6 0.0 copy-done
  159.6 1.1 copy.15
  160.7 0.0 copy-done.1
  160.7 0.6 copy.16
Async XLA Ops:
  155.7 3.9 %copy-start = (f32[384,1024]{1,0:T(8,128)S(1)}, f32[384,1024]{1,0:T(8,128)}, u32[]{:S(2)}) copy-start(f32[384,1024]{1,0:T(8,128)} %get-tuple-element.29) | copy-start | bytes 4718596
  155.7 5.0 %copy-start.1 = (f32[16,128]{1,0:T(8,128)S(1)}, f32[16,128]{1,0:T(8,128)}, u32[]{:S(2)}) copy-start(f32[16,128]{1,0:T(8,128)} %get-tuple-element.24) | copy-start | bytes 24580

commit v3 on v2

v3 whole, which is shorter than its diff:
```python
import functools

import jax
import jax.numpy as jnp
from jax import lax
from jax.experimental import pallas as pl
from jax.experimental.pallas import tpu as pltpu
from jax.sharding import PartitionSpec as P

MESH = pl.DeviceIdType.MESH
F32 = jnp.float32
BF16 = jnp.bfloat16
I32 = jnp.int32

CAP = 12
HALF = CAP // 2
COLS = 256
GROUP = 16
GROUPS = 80
STRIDE = 27

ROW_SEND = 0
ROW_PERM = 12
ROW_SLOT = 22
ROW_LAST = 23
ROW_RET = 28
ROW_LINK = 32
ROW_FIRST = 40
ROW_ONE = 42
ROW_TWO = 44
ROW_PART = 46
ROW_POS = 52
ROW_PERM_W = 64
TAB_ROWS = 80
CHUNK = 4096
PARTS = 3


def iota(shape, dim):
    return lax.broadcasted_iota(I32, shape, dim)


def one(mask):
    return jnp.where(mask, 1.0, 0.0).astype(BF16)


def mm(left, right):
    return jnp.dot(left, right, preferred_element_type=F32)


def mm_tn(left, right):
    return lax.dot_general(left, right, (((0,), (0,)), ((), ())), preferred_element_type=F32)


def mm_nt(left, right):
    return lax.dot_general(left, right, (((1,), (1,)), ((), ())), preferred_element_type=F32)


def to_col(row, n):
    eye = iota((n, n), 0) == iota((n, n), 1)
    return jnp.sum(jnp.where(eye, jnp.broadcast_to(row, (n, n)), 0.0), axis=1, keepdims=True)


def to_row(col, n):
    eye = iota((n, n), 0) == iota((n, n), 1)
    return jnp.sum(jnp.where(eye, jnp.broadcast_to(col, (n, n)), 0.0), axis=0, keepdims=True)


def put(tab_ref, row, values):
    width = values.shape[1]
    tab_ref[row : row + 1, :] = values[:, :128]
    tab_ref[row + 1 : row + 2, : width - 128] = values[:, 128:]


def index_kernel(
    devs, genes, paths, mem_ref, slot_ref, len_ref, link_ref, tab_ref, rows_ref,
    s_ref, own_ref, tile_ref,
):
    me = lax.axis_index("genes")
    per = genes
    table = slot_ref[...]
    halves = jnp.concatenate([table >> 5, table & 31], axis=0).astype(F32).astype(BF16)
    rows = table.shape[0]
    pair = 2 * per

    for m in range(2):
        def look(j, _, m=m):
            q = mem_ref[m : m + 1, pl.ds(pl.multiple_of(j * pair, 128), pair)]
            lane = q & 127
            which = q >> 7
            hot = one(jnp.broadcast_to(lane, (128, pair)) == iota((128, pair), 0))
            vals = mm(halves, hot)
            pick = jnp.broadcast_to(which, (rows, pair)) == iota((rows, pair), 0)
            owner = jnp.sum(jnp.where(pick, vals[:rows], 0.0), axis=0, keepdims=True)
            local = jnp.sum(jnp.where(pick, vals[rows:], 0.0), axis=0, keepdims=True)
            slot = owner * 32.0 + local
            s_ref[pl.ds(m * devs + 2 * j, 1), :] = slot[:, :per]
            s_ref[pl.ds(m * devs + 2 * j + 1, 1), :] = slot[:, per:]
            return 0

        lax.fori_loop(0, devs // 2, look, 0, unroll=4)

    tab_ref[...] = jnp.zeros((TAB_ROWS, 128), I32)
    slots = s_ref[...].astype(I32)
    mine = (slots >> 5) == me
    local = (slots & 31).astype(F32)
    upper = one(iota((per, per), 0) < iota((per, per), 1))
    before = mm(one(mine), upper)
    count = jnp.sum(jnp.where(mine, 1.0, 0.0), axis=1, keepdims=True)
    lead = jnp.concatenate([jnp.zeros((devs, 1), F32), count[:devs]], axis=0)
    rank = before + lead
    lower = one(iota((devs, devs), 1) < iota((devs, devs), 0))
    lane64 = iota((devs, 128), 1)
    carry = jnp.zeros((1, 128), F32)
    places, cells = [], []
    for r in range(CAP):
        hit = mine & (rank == float(r))
        got = jnp.sum(jnp.where(hit, local + 1.0, 0.0), axis=1, keepdims=True)
        got = got[:devs] + got[devs:]
        cell = jnp.where(got == 0.0, float(paths), got - 1.0).astype(I32)
        hot = jnp.broadcast_to(cell, (devs, 128)) == lane64
        within = mm(lower, one(hot)) + carry
        carry = carry + jnp.sum(jnp.where(hot, 1.0, 0.0), axis=0, keepdims=True)
        places.append(jnp.sum(jnp.where(hot, within, 0.0), axis=1, keepdims=True))
        cells.append(hot)
    lane1 = iota((1, 128), 1)
    groups = jnp.where(lane1 < paths, ((carry.astype(I32) + (GROUP - 1)) // GROUP).astype(F32), 0.0)
    strict = one(iota((128, 128), 0) < iota((128, 128), 1))
    start = mm(jnp.broadcast_to(groups.astype(BF16), (8, 128)), strict)[:1]
    end_col = to_col(start + groups, 128)
    ends = jnp.where(
        (jnp.broadcast_to(end_col, (128, 128)) <= iota((128, 128), 1).astype(F32))
        & (iota((128, 128), 0) < paths),
        1.0,
        0.0,
    )
    tab_ref[ROW_SLOT : ROW_SLOT + 1, :] = jnp.sum(ends, axis=0, keepdims=True).astype(I32)
    final = jnp.where(groups > 0.0, start + groups - 1.0, float(GROUPS))
    tab_ref[ROW_LAST : ROW_LAST + 1, :] = final.astype(I32)
    src_sum = jnp.zeros((16, 128), F32)
    rank_sum = jnp.zeros((16, 128), F32)
    link_sum = jnp.zeros((16, 128), F32)
    seen = jnp.zeros((16, 128), F32)
    source = iota((devs, 128), 0).astype(F32).astype(BF16)
    for r in range(CAP):
        first = jnp.sum(
            jnp.where(cells[r], jnp.broadcast_to(start, (devs, 128)), 0.0), axis=1, keepdims=True
        )
        real = jnp.sum(jnp.where(cells[r] & (lane64 < paths), 1.0, 0.0), axis=1, keepdims=True)
        pos = first * float(GROUP) + places[r]
        tab_ref[ROW_POS + r : ROW_POS + r + 1, :devs] = to_row(
            jnp.where(real > 0.0, pos, 0.0), devs
        ).astype(I32)
        pos = jnp.where(real > 0.0, pos.astype(I32), 1 << 20)
        high = one(jnp.broadcast_to(pos >> 7, (devs, 16)) == iota((devs, 16), 1))
        low = jnp.broadcast_to(pos & 127, (devs, 128)) == lane64
        src_sum = src_sum + mm_tn(high, jnp.where(low, source, jnp.zeros((), BF16)))
        found = mm_tn(high, one(low))
        rank_sum = rank_sum + found * float(r)
        link_sum = link_sum + found * float(r if r < HALF else r + (devs - 1) * HALF)
        seen = seen + found
    perm = jnp.where(seen > 0.0, src_sum * float(CAP) + rank_sum, float(devs * CAP))
    tab_ref[ROW_PERM : ROW_PERM + 10, :] = perm.astype(I32)[:10]
    perm = jnp.where(seen > 0.0, src_sum * float(HALF) + link_sum, float(devs * CAP))
    tab_ref[ROW_PERM_W : ROW_PERM_W + 10, :] = perm.astype(I32)[:10]

    own_ref[0:1, :] = s_ref[pl.ds(me, 1), :]
    own_ref[1:2, :] = s_ref[pl.ds(devs + me, 1), :]
    lower_g = one(iota((per, per), 1) < iota((per, per), 0))
    lane_g = iota((per, 128), 1)
    gene_col = iota((per, 128), 0).astype(F32).astype(BF16)
    carry = jnp.zeros((1, 128), F32)
    send = jnp.zeros((16, 128), F32)
    owner_rows = [own_ref[m : m + 1, :].astype(I32) >> 5 for m in range(2)]
    for m in range(2):
        owner = (to_col(own_ref[m : m + 1, :], per).astype(I32)) >> 5
        hot = jnp.broadcast_to(owner, (per, 128)) == lane_g
        within = mm(lower_g, one(hot)) + carry
        carry = carry + jnp.sum(jnp.where(hot, 1.0, 0.0), axis=0, keepdims=True)
        order = jnp.sum(jnp.where(hot, within, 0.0), axis=1, keepdims=True)
        cell = one(jnp.broadcast_to(order, (per, 16)) == iota((per, 16), 1).astype(F32))
        send = send + 2.0 * mm_tn(cell, jnp.where(hot, gene_col, jnp.zeros((), BF16)))
        if m:
            send = send + mm_tn(cell, one(hot))
        owner_row = owner_rows[m]
        order_row = to_row(order, per).astype(I32)
        put(tab_ref, ROW_RET + 2 * m, owner_row * CAP + order_row)
        link_row = owner_row * HALF + order_row
        link_row = jnp.where(order_row < HALF, link_row, link_row + (devs - 1) * HALF)
        put(tab_ref, ROW_LINK + 2 * m, link_row)
    tab_ref[ROW_SEND : ROW_SEND + CAP, :] = send.astype(I32)[:CAP]

    lens = len_ref[...].astype(F32) - 128.0
    starts = mm(jnp.broadcast_to(lens.astype(BF16), (8, per)), upper)[:1]
    starts = starts + 128.0 * iota((1, per), 1).astype(F32)
    start_col = jnp.broadcast_to(to_col(starts, per), (per, 256))
    begin = (iota((per, 256), 1) * COLS).astype(F32)
    inside = jnp.where(start_col <= begin, 1.0, 0.0)
    put(tab_ref, ROW_FIRST, (jnp.sum(inside, axis=0, keepdims=True) - 1.0).astype(I32))
    end = float(per * COLS)
    next_one = jnp.min(jnp.where(start_col > begin, start_col, end), axis=0, keepdims=True)
    next_two = jnp.min(
        jnp.where(start_col > jnp.broadcast_to(next_one, (per, 256)), start_col, end),
        axis=0, keepdims=True,
    )
    put(tab_ref, ROW_ONE, (next_one - begin[:1]).astype(I32))
    put(tab_ref, ROW_TWO, (next_two - begin[:1]).astype(I32))
    start_col = start_col[:, :per]
    starts_i = starts.astype(I32)
    last = (starts_i + len_ref[...] - 1) >> 8
    gene_row = iota((1, per), 1)
    for j in range(PARTS):
        block = (starts_i >> 8) + j
        edge = jnp.broadcast_to((block * COLS).astype(F32), (per, per))
        under = jnp.where(start_col <= edge, 1.0, 0.0)
        lead_gene = jnp.sum(under, axis=0, keepdims=True).astype(I32) - 1
        row = block * PARTS + (gene_row - lead_gene)
        put(tab_ref, ROW_PART + 2 * j, jnp.where(block <= last, row, per * PARTS))

    def relayout(e, _):
        at = pl.multiple_of(16 * e, 16)
        rows = link_ref[pl.ds(at, 16), :].astype(F32)
        for n in range(2):
            for t in range(8):
                tile_ref[pl.ds(64 * n + t, 8, stride=8), :] = rows[
                    8 * n : 8 * n + 8, 128 * t : 128 * t + 128
                ]
        for n in range(16):
            rows_ref[at + n] = tile_ref[8 * n : 8 * n + 8, :].astype(BF16)
        return 0

    lax.fori_loop(0, link_ref.shape[0] // 16, relayout, 0)


def look_up(tab_ref, row, index):
    return tab_ref[row + (index >> 7), index & 127]


def window_of(tab_ref, block):
    return tuple(look_up(tab_ref, row, block) for row in (ROW_FIRST, ROW_ONE, ROW_TWO))


def partner(me, k):
    off = lax.rem(k * STRIDE, 64)
    x = lax.rem(me // 16 + off // 16, 4)
    z = lax.rem((me // 4) % 4 + (off // 4) % 4, 4)
    y = lax.rem(me % 4 + off % 4, 4)
    return x * 16 + z * 4 + y


def greet(devs, me, core):
    barrier = pltpu.get_barrier_semaphore()

    def hello(k, _):
        pl.semaphore_signal(
            barrier, inc=1, device_id=(partner(me, k), core), device_id_type=MESH
        )
        return 0

    lax.fori_loop(1, devs, hello, 0)
    pl.semaphore_signal(barrier, inc=1, device_id=(me, 1 - core), device_id_type=MESH)
    pl.semaphore_wait(barrier, devs)


def load_chunks(src_ref, dst_ref, sem):
    return [
        pltpu.make_async_copy(
            src_ref.at[:, pl.ds(c * CHUNK, CHUNK)], dst_ref.at[:, pl.ds(c * CHUNK, CHUNK)], sem.at[c]
        )
        for c in range(src_ref.shape[1] // CHUNK)
    ]


def main_kernel(
    devs, genes, units, paths, punits,
    tab_ref, link_ref, head_ref, cot_ref, geno_ref, weight_ref,
    out_ref, path_ref, gh_ref,
    g_ref, gsib_ref, gw_ref, hid_ref, h_ref, w_ref, hs_ref, ws_ref, he_ref, wl_ref, gp_ref,
    hd_ref, delta_ref, heads_ref, own_gh, sib_gh, give_ref, take_ref, back_ref, lrow_ref,
    own_ref, sib_ref, grad_ref, tile_ref,
    geno_sem, weight_sem, out_sem, hsend, hrecv, wsend, wrecv, dsend, drecv, lsend, lrecv, pair_sem,
):
    me = lax.axis_index("genes")
    core = lax.axis_index("batch")
    low = core * HALF
    high = (1 - core) * HALF
    samples = geno_ref.shape[0]
    half = units // 2
    tiles = punits // 8
    span = geno_ref.shape[1] // 2
    here = pl.multiple_of(core * span, span)
    there = pl.multiple_of((1 - core) * span, span)
    flat = pl.ds(0, (devs - 1) * CAP)
    flat_half = pl.ds(0, (devs - 1) * HALF)
    mine = core * (devs * HALF)
    loads = load_chunks(geno_ref, g_ref, geno_sem)
    weights = load_chunks(weight_ref, gw_ref, weight_sem)
    for weight, load in zip(weights, loads):
        weight.start()
        load.start()
    greet(devs, me, core)

    def send(src, dst, send_sem, recv_sem, to):
        return pltpu.make_async_remote_copy(
            src_ref=src, dst_ref=dst, send_sem=send_sem, recv_sem=recv_sem,
            device_id=(to, core), device_id_type=MESH,
        )

    def pair(src, dst, n):
        return pltpu.make_async_remote_copy(
            src_ref=src, dst_ref=dst, send_sem=pair_sem.at[2 * n], recv_sem=pair_sem.at[2 * n + 1],
            device_id=(me, 1 - core), device_id_type=MESH,
        )

    def w_step(k, _):
        to = partner(me, k)
        for r in range(HALF):
            ws_ref[to * HALF + r] = link_ref[tab_ref[low + r, to]]
        send(
            ws_ref.at[pl.ds(to * HALF, HALF)], w_ref.at[pl.ds(mine + me * HALF, HALF)],
            wsend, wrecv, to,
        ).start()
        return 0

    lax.fori_loop(1, devs, w_step, 0)

    pos = iota((units, COLS), 1)
    for n in range(2):
        gp_ref[2 * genes * PARTS + n] = jnp.zeros((8, 128), F32)
    per_chunk = CHUNK // COLS
    for c, load in enumerate(loads):
        weights[c].wait()
        load.wait()

        def block(i, _, c=c):
            for k in range(4):
                b = c * per_chunk + i * 4 + k
                _, one_end, two_end = window_of(tab_ref, b)
                cols = pl.ds(pl.multiple_of(b * COLS, COLS), COLS)
                weight = gw_ref[:, cols].astype(F32)
                not_one = pos >= one_end
                not_two = pos >= two_end
                zero = jnp.zeros_like(weight)
                basis = jnp.concatenate(
                    [
                        jnp.where(not_one, zero, weight),
                        jnp.where(not_one & jnp.logical_not(not_two), weight, zero),
                        jnp.where(not_two, weight, zero),
                    ],
                    axis=0,
                ).astype(BF16)
                got = mm_nt(basis, g_ref[:, cols])
                for w in range(2 * PARTS):
                    gp_ref[b * 2 * PARTS + w] = got[8 * w : 8 * w + 8]
            return 0

        lax.fori_loop(0, per_chunk // 4, block, 0)
    geno = pair(g_ref.at[:, pl.ds(there, span)], gsib_ref, 0)
    geno.start()

    def finish(i, _):
        for k in range(8):
            at = [2 * look_up(tab_ref, ROW_PART + 2 * j, i * 8 + k) for j in range(PARTS)]
            for n in range(2):
                total = gp_ref[at[0] + n] + gp_ref[at[1] + n] + gp_ref[at[2] + n]
                tile_ref[k * units + 8 * n : k * units + 8 * n + 8, :] = jnp.tanh(total)
        for k in range(8):
            even = tile_ref[pl.ds(k * units, half, stride=2), :]
            odd = tile_ref[pl.ds(k * units + 1, half, stride=2), :]
            hid_ref[i * 8 + k] = jnp.concatenate([even, odd], axis=1).astype(BF16)
        return 0

    lax.fori_loop(0, genes // 8, finish, 0)

    def h_step(k, _):
        to = partner(me, k)
        for r in range(CAP):
            hs_ref[to * CAP + r] = hid_ref[tab_ref[r, to] >> 1]
        send(
            hs_ref.at[pl.ds(to * CAP, CAP)], h_ref.at[pl.ds(me * CAP, CAP)], hsend, hrecv, to
        ).start()
        return 0

    lax.fori_loop(1, devs, h_step, 0)
    for r in range(CAP):
        h_ref[me * CAP + r] = hid_ref[tab_ref[r, me] >> 1]
    for r in range(HALF):
        w_ref[mine + me * HALF + r] = link_ref[tab_ref[low + r, me]]
    h_ref[devs * CAP] = jnp.zeros(h_ref.shape[1:], BF16)
    w_ref[devs * CAP] = jnp.zeros(w_ref.shape[1:], BF16)
    send(ws_ref.at[flat_half], w_ref.at[flat_half], wsend, wrecv, me).wait()
    part = w_ref.at[pl.ds(mine, devs * HALF)]
    share = pair(part, part, 8 + span // CHUNK)
    share.start()
    share.wait()

    def gather_w(i, _):
        for q in range(128 // GROUP):
            for j in range(GROUP):
                wl_ref[i * (128 // GROUP) + q, 8 * j : 8 * j + 8, :] = w_ref[
                    tab_ref[ROW_PERM_W + i, q * GROUP + j]
                ]
        return 0

    lax.fori_loop(0, GROUPS * GROUP // 128, gather_w, 0)
    heads_ref[...] = head_ref[...].astype(F32)
    for t in range(tiles):
        gp_ref[GROUPS * tiles + t] = jnp.zeros((8, 128), F32)
    delta_ref[paths] = jnp.zeros((punits, 128), BF16)
    for n in range(genes, own_ref.shape[0]):
        own_ref[n] = jnp.zeros((units, 128), BF16)
        sib_ref[n] = jnp.zeros((units, 128), BF16)
    send(hs_ref.at[flat], h_ref.at[flat], hsend, hrecv, me).wait()

    def up(i, carry):
        for q in range(128 // GROUP):
            c = i * (128 // GROUP) + q
            for j in range(GROUP):
                p = tab_ref[ROW_PERM + i, q * GROUP + j]
                he_ref[c, 8 * j : 8 * j + 8, :] = h_ref[p]
            out = mm_tn(wl_ref[c], he_ref[c])
            out = out[:punits, :128] + out[punits:, 128:]
            slot = tab_ref[ROW_SLOT, c]
            prev, total = carry
            total = out + jnp.where(slot == prev, total, jnp.zeros_like(total))
            for t in range(tiles):
                gp_ref[c * tiles + t] = total[8 * t : 8 * t + 8]
            carry = (slot, total)
        return carry

    lax.fori_loop(
        0, GROUPS * GROUP // 128, up, (jnp.full((), -1, I32), jnp.zeros((punits, 128), F32))
    )

    cot = cot_ref[...]
    lane = iota((punits, 128), 1)
    sub = iota((punits, 128), 0)

    def middle(i, _):
        row = jnp.zeros((1, 128), F32)
        head_row = heads_ref[pl.ds(i, 1), :]
        for n in range(2):
            s = 2 * i + n
            at = tab_ref[ROW_LAST, s] * tiles
            active = jnp.tanh(
                jnp.concatenate([gp_ref[at + t] for t in range(tiles)], axis=0)
            )
            diag = lane == sub + punits * n
            head = jnp.sum(
                jnp.where(diag, jnp.broadcast_to(head_row, (punits, 128)), 0.0),
                axis=1, keepdims=True,
            )
            grad = jnp.sum(active * cot, axis=1, keepdims=True)
            row = row + jnp.sum(
                jnp.where(diag, jnp.broadcast_to(grad, (punits, 128)), 0.0), axis=0, keepdims=True
            )
            delta_ref[s] = (cot * head * (1.0 - active * active)).astype(BF16)
        own_gh[pl.ds(i, 1), :] = row
        return 0

    lax.fori_loop(0, paths // 2, middle, 0)

    def down(i, _):
        for q in range(4):
            c = i * 4 + q
            delta = delta_ref[tab_ref[ROW_SLOT, c]]
            none = jnp.zeros_like(delta)
            wide = jnp.concatenate(
                [
                    jnp.concatenate([delta, none], axis=1),
                    jnp.concatenate([none, delta], axis=1),
                ],
                axis=0,
            )
            gp = mm_nt(he_ref[c], wide)
            hd = mm(wl_ref[c], wide).astype(BF16)
            for j in range(GROUP):
                gp_ref[c * GROUP + j] = gp[8 * j : 8 * j + 8]
                hd_ref[c * GROUP + j] = hd[8 * j : 8 * j + 8]
        return 0

    lax.fori_loop(0, GROUPS // 4, down, 0)

    def d_step(k, _):
        to = partner(me, k)
        for r in range(CAP):
            hs_ref[to * CAP + r] = hd_ref[tab_ref[ROW_POS + r, to]]
        send(
            hs_ref.at[pl.ds(to * CAP, CAP)], back_ref.at[pl.ds(me * CAP, CAP)], dsend, drecv, to
        ).start()
        return 0

    lax.fori_loop(1, devs, d_step, 0)

    def give_step(i, _):
        for r in range(HALF):
            give_ref[i * HALF + r] = gp_ref[tab_ref[ROW_POS + high + r, i]]
        return 0

    lax.fori_loop(0, devs, give_step, 0)
    parts = pair(give_ref, take_ref, 1)
    parts.start()
    swap = pair(own_gh, sib_gh, 2)
    swap.start()
    for r in range(CAP):
        back_ref[me * CAP + r] = hd_ref[tab_ref[ROW_POS + r, me]]
    parts.wait()

    def l_step(k, _):
        to = partner(me, k)
        for r in range(HALF):
            ws_ref[to * HALF + r] = (
                gp_ref[tab_ref[ROW_POS + low + r, to]] + take_ref[to * HALF + r]
            ).astype(BF16)
        send(
            ws_ref.at[pl.ds(to * HALF, HALF)], lrow_ref.at[pl.ds(mine + me * HALF, HALF)],
            lsend, lrecv, to,
        ).start()
        return 0

    lax.fori_loop(1, devs, l_step, 0)
    for r in range(HALF):
        lrow_ref[mine + me * HALF + r] = (
            gp_ref[tab_ref[ROW_POS + low + r, me]] + take_ref[me * HALF + r]
        ).astype(BF16)
    swap.wait()
    gh_ref[...] = own_gh[...] + sib_gh[...]
    send(hs_ref.at[flat], back_ref.at[flat], dsend, drecv, me).wait()

    def gene(i, _):
        for k in range(4):
            g = 4 * i + k
            a = look_up(tab_ref, ROW_RET, g)
            b = look_up(tab_ref, ROW_RET + 2, g)
            both = back_ref[a].astype(F32) + back_ref[b].astype(F32)
            hid = hid_ref[g].astype(F32)
            value = both * (1.0 - hid * hid)
            tile_ref[pl.ds(k * units, half, stride=2), :] = value[:, :128]
            tile_ref[pl.ds(k * units + 1, half, stride=2), :] = value[:, 128:]
        for k in range(4):
            own_ref[4 * i + k] = tile_ref[k * units : (k + 1) * units, :].astype(BF16)
        return 0

    quarter = genes // 4
    deltas = []
    for n in range(4):
        lax.fori_loop(n * quarter // 4, (n + 1) * quarter // 4, gene, 0)
        rows = pl.ds(n * quarter, quarter)
        delta = pair(own_ref.at[rows], sib_ref.at[rows], 4 + n)
        delta.start()
        deltas.append(delta)
    geno.wait()
    for delta in deltas:
        delta.wait()

    stores = []
    first_block = core * (span // COLS)
    for c in range(span // CHUNK):
        def block(i, _, c=c):
            for k in range(4):
                b = c * per_chunk + i * 4 + k
                first, one_end, two_end = window_of(tab_ref, first_block + b)
                left = jnp.concatenate(
                    [
                        jnp.concatenate([ref[first + w] for w in range(PARTS)], axis=0)
                        for ref in (own_ref, sib_ref)
                    ],
                    axis=1,
                )
                cols = pl.ds(pl.multiple_of(b * COLS, COLS), COLS)
                whole = pl.ds(pl.multiple_of(here + b * COLS, COLS), COLS)
                right = jnp.concatenate([g_ref[:, whole], gsib_ref[:, cols]], axis=0)
                full = mm(left, right)
                grad_ref[:, cols] = jnp.where(
                    pos >= two_end,
                    full[2 * units :],
                    jnp.where(pos >= one_end, full[units : 2 * units], full[:units]),
                )
            return 0

        lax.fori_loop(0, per_chunk // 4, block, 0)
        cols = pl.ds(pl.multiple_of(here + c * CHUNK, CHUNK), CHUNK)
        piece = grad_ref.at[:, pl.ds(c * CHUNK, CHUNK)]
        store = pltpu.make_async_copy(piece, out_ref.at[:, cols], out_sem.at[c])
        store.start()
        stores.append(store)
        store = pair(piece, out_ref.at[:, cols], 8 + c)
        store.start()
        stores.append(store)

    send(ws_ref.at[flat_half], lrow_ref.at[flat_half], lsend, lrecv, me).wait()
    part = lrow_ref.at[pl.ds(mine, devs * HALF)]
    share = pair(part, part, 3)
    share.start()
    share.wait()

    def link_group(e, _):
        for j in range(8):
            g = e * 4 + j // 2
            at = look_up(tab_ref, ROW_LINK + 2 * (j % 2), g)
            tile_ref[8 * j : 8 * j + 8, :] = lrow_ref[at].astype(F32)
        for t in range(8):
            path_ref[pl.ds(pl.multiple_of(8 * e, 8), 8), 128 * t : 128 * t + 128] = tile_ref[
                pl.ds(t, 8, stride=8), :
            ]
        return 0

    lax.fori_loop(0, path_ref.shape[0] // 8, link_group, 0)
    for store in stores:
        store.wait()


def vmem():
    return pl.BlockSpec(memory_space=pltpu.VMEM)


def smem():
    return pl.BlockSpec(memory_space=pltpu.SMEM)


def hbm():
    return pl.BlockSpec(memory_space=pl.ANY)


LIMIT = 60 * 1024 * 1024


def on_device(
    genotypes, gene_weight, gene_lengths, membership, pathway_slot, pathway_weight,
    head_weight, cotangent,
):
    devs = lax.axis_size("genes")
    genes = gene_lengths.shape[0]
    links = pathway_weight.shape[0]
    units = gene_weight.shape[0]
    samples, variants = genotypes.shape
    punits = pathway_weight.shape[1] // units
    paths = head_weight.shape[0] // punits
    half = units // 2
    shape = jax.ShapeDtypeStruct

    tab, link_rows = pl.pallas_call(
        functools.partial(index_kernel, devs, genes, paths),
        out_shape=(
            shape((TAB_ROWS, 128), I32),
            shape((links, half, 2 * punits), BF16),
        ),
        in_specs=[vmem()] * 4,
        out_specs=(vmem(),) * 2,
        scratch_shapes=[
            pltpu.VMEM((2 * devs, genes), F32),
            pltpu.VMEM((2, genes), F32),
            pltpu.VMEM((128, 128), F32),
        ],
        compiler_params=pltpu.CompilerParams(vmem_limit_bytes=LIMIT),
        name="index",
    )(membership.T, pathway_slot.reshape(-1, 128), gene_lengths.reshape(1, -1), pathway_weight)

    pieces = variants // CHUNK
    sem = pltpu.SemaphoreType.DMA
    heads = (paths * punits // 128, 128)
    tile = lambda n, width, kind: pltpu.VMEM((n, half, width), kind)
    grad_gene, grad_pathway, grad_head = pl.pallas_call(
        functools.partial(main_kernel, devs, genes, units, paths, punits),
        out_shape=(
            shape((units, variants), F32),
            shape((links, units * punits), F32),
            shape(heads, F32),
        ),
        in_specs=[smem()] + [vmem()] * 3 + [hbm()] * 2,
        out_specs=(hbm(), vmem(), vmem()),
        scratch_shapes=[
            pltpu.VMEM((samples, variants), BF16),
            pltpu.VMEM((samples, variants // 2), BF16),
            pltpu.VMEM((units, variants), BF16),
            tile(genes, 2 * samples, BF16),
            tile(devs * CAP + 1, 2 * samples, BF16),
            tile(devs * CAP + 1, 2 * punits, BF16),
            tile(devs * CAP, 2 * samples, BF16),
            tile(devs * HALF, 2 * punits, BF16),
            pltpu.VMEM((GROUPS, half * GROUP, 2 * samples), BF16),
            pltpu.VMEM((GROUPS, half * GROUP, 2 * punits), BF16),
            tile(GROUPS * GROUP, 2 * punits, F32),
            tile(GROUPS * GROUP, 2 * samples, BF16),
            pltpu.VMEM((paths + 1, punits, samples), BF16),
            pltpu.VMEM(heads, F32),
            pltpu.VMEM(heads, F32),
            pltpu.VMEM(heads, F32),
            tile(devs * HALF, 2 * punits, F32),
            tile(devs * HALF, 2 * punits, F32),
            tile(devs * CAP, 2 * samples, BF16),
            tile(devs * CAP, 2 * punits, BF16),
            pltpu.VMEM((genes + 2, units, samples), BF16),
            pltpu.VMEM((genes + 2, units, samples), BF16),
            pltpu.VMEM((units, variants // 2), F32),
            pltpu.VMEM((8 * units, samples), F32),
        ]
        + [sem((pieces,))] * 2
        + [sem((pieces // 2,))]
        + [sem(())] * 8
        + [sem((18 + pieces,))],
        compiler_params=pltpu.CompilerParams(
            collective_id=0, has_side_effects=True, vmem_limit_bytes=66_000_000
        ),
        name="main",
    )(
        tab,
        link_rows,
        head_weight.reshape(-1, 128),
        cotangent.reshape(1, -1),
        genotypes,
        gene_weight,
    )
    return grad_gene, grad_pathway, grad_head.reshape(-1)


def solution(mesh):
    return jax.shard_map(
        on_device,
        mesh=mesh,
        in_specs=(
            P("batch", "genes"), P(None, "genes"), P("genes"), P(), P(),
            P("genes", None), P("genes"), P("batch"),
        ),
        out_specs=(P(None, "genes"), P("genes", None), P("genes")),
        check_vma=False,
    )
```

time: 161 us -> 147 us (0.913)
  Pallas kernels: 155 us -> 140 us
    pallas_call x3 -> x1, Pallas kernels: 146 us -> 131 us  [on_device(): pl.pallas_call(functools.partial(main_kernel, devs, genes, units, paths,...]
where the time goes in v3:
time: 147 us
  Pallas kernels  140 us (95%)
  local copies, waits for them, and re-layouts  5.62 us (4%)
    pallas_call x1, Pallas kernels, on_device(): pl.pallas_call(functools.partial(main_kernel, devs, genes, units, paths,...  131 us
    pallas_call x1, Pallas kernels, on_device(): pl.pallas_call(functools.partial(index_kernel, devs, genes, paths), out_s...  9.18 us
    unnamed x7, local copies, waits for them, and re-layouts  5.62 us

profile of v3, /device:TPU:1, one launch (start us, length us, event | category | flops | bytes accessed | tf_op | source)
XLA Modules:
  0.0 146.5 jit_solution(11190997332068425806)
XLA Ops:
  0.6 9.2 %index.1 = (s32[80,128]{1,0:T(8,128)}, bf16[384,8,128]{2,1,0:T(8,128)(2,1)}) custom-call(s32[2,12288]{1,0:T(2,128)} %bitcast.6, s32[16,128]{1,0:T(8,128)} %bitcast.7, s32[1,192]{1,0:T(1,128)} %bitcast.10, bf16[384,1024]{1,0:T(8,128)(2,1)} %link_ref.1), custom_call_target="tpu_custom_call" | custom-call | tf_op jit(solution)/shard_map/index/pallas_call | solution.py:642
  9.8 131.1 %main.1 = (f32[16,49152]{1,0:T(8,128)}, f32[384,1024]{1,0:T(8,128)}, f32[16,128]{1,0:T(8,128)}) custom-call(s32[80,128]{1,0:T(8,128)} %get-tuple-element.8.tab_ref, bf16[384,8,128]{2,1,0:T(8,128)(2,1)} %get-tuple-element.9.link_ref, bf16[16,128]{1,0:T(8,128)(2,1)} %bitcast.9, f32[1,128]{1,0:T(1,128)} %bitcast.11, bf16[128,49152]{1,0:T(8,128)(2,1)} %geno_ref.1, ...), custom_call_target="tpu_custom_call" | custom-call | tf_op jit(solution)/shard_map/main/pallas_call | solution.py:663
  140.9 0.0 copy-start
  140.9 0.0 copy-start.1
  140.9 3.9 %copy.14 = f32[16,49152]{1,0:T(8,128)} copy(f32[16,49152]{1,0:T(8,128)} %get-tuple-element.16) | data formatting | bytes 6291456
  144.8 0.0 copy-done
  144.8 1.1 copy.15
  145.9 0.0 copy-done.1
  145.9 0.6 copy.16
Async XLA Ops:
  140.9 3.9 %copy-start = (f32[384,1024]{1,0:T(8,128)S(1)}, f32[384,1024]{1,0:T(8,128)}, u32[]{:S(2)}) copy-start(f32[384,1024]{1,0:T(8,128)} %get-tuple-element.17) | copy-start | bytes 4718596
  140.9 5.0 %copy-start.1 = (f32[16,128]{1,0:T(8,128)S(1)}, f32[16,128]{1,0:T(8,128)}, u32[]{:S(2)}) copy-start(f32[16,128]{1,0:T(8,128)} %get-tuple-element.12) | copy-start | bytes 24580

commit v4 on v3

--- a/solution.py
+++ b/solution.py
@@ -257,7 +257,7 @@
         )
         return 0
 
-    lax.fori_loop(1, devs, hello, 0)
+    lax.fori_loop(1, devs, hello, 0, unroll=3)
     pl.semaphore_signal(barrier, inc=1, device_id=(me, 1 - core), device_id_type=MESH)
     pl.semaphore_wait(barrier, devs)
 
@@ -274,9 +274,9 @@
 def main_kernel(
     devs, genes, units, paths, punits,
     tab_ref, link_ref, head_ref, cot_ref, geno_ref, weight_ref,
-    out_ref, path_ref, gh_ref,
+    out_ref, lrow_ref, gh_ref,
     g_ref, gsib_ref, gw_ref, hid_ref, h_ref, w_ref, hs_ref, ws_ref, he_ref, wl_ref, gp_ref,
-    hd_ref, delta_ref, heads_ref, own_gh, sib_gh, give_ref, take_ref, back_ref, lrow_ref,
+    hd_ref, delta_ref, heads_ref, own_gh, sib_gh, give_ref, take_ref, back_ref,
     own_ref, sib_ref, grad_ref, tile_ref,
     geno_sem, weight_sem, out_sem, hsend, hrecv, wsend, wrecv, dsend, drecv, lsend, lrecv, pair_sem,
 ):
@@ -322,7 +322,7 @@
         ).start()
         return 0
 
-    lax.fori_loop(1, devs, w_step, 0)
+    lax.fori_loop(1, devs, w_step, 0, unroll=3)
 
     pos = iota((units, COLS), 1)
     for n in range(2):
@@ -460,22 +460,22 @@
 
     lax.fori_loop(0, paths // 2, middle, 0)
 
+    def wide_of(c):
+        delta = delta_ref[tab_ref[ROW_SLOT, c]]
+        none = jnp.zeros_like(delta)
+        return jnp.concatenate(
+            [
+                jnp.concatenate([delta, none], axis=1),
+                jnp.concatenate([none, delta], axis=1),
+            ],
+            axis=0,
+        )
+
     def down(i, _):
         for q in range(4):
             c = i * 4 + q
-            delta = delta_ref[tab_ref[ROW_SLOT, c]]
-            none = jnp.zeros_like(delta)
-            wide = jnp.concatenate(
-                [
-                    jnp.concatenate([delta, none], axis=1),
-                    jnp.concatenate([none, delta], axis=1),
-                ],
-                axis=0,
-            )
-            gp = mm_nt(he_ref[c], wide)
-            hd = mm(wl_ref[c], wide).astype(BF16)
+            hd = mm(wl_ref[c], wide_of(c)).astype(BF16)
             for j in range(GROUP):
-                gp_ref[c * GROUP + j] = gp[8 * j : 8 * j + 8]
                 hd_ref[c * GROUP + j] = hd[8 * j : 8 * j + 8]
         return 0
 
@@ -491,6 +491,16 @@
         return 0
 
     lax.fori_loop(1, devs, d_step, 0)
+
+    def down_links(i, _):
+        for q in range(4):
+            c = i * 4 + q
+            gp = mm_nt(he_ref[c], wide_of(c))
+            for j in range(GROUP):
+                gp_ref[c * GROUP + j] = gp[8 * j : 8 * j + 8]
+        return 0
+
+    lax.fori_loop(0, GROUPS // 4, down_links, 0)
 
     def give_step(i, _):
         for r in range(HALF):
@@ -594,20 +604,49 @@
     share.start()
     share.wait()
 
-    def link_group(e, _):
-        for j in range(8):
-            g = e * 4 + j // 2
-            at = look_up(tab_ref, ROW_LINK + 2 * (j % 2), g)
-            tile_ref[8 * j : 8 * j + 8, :] = lrow_ref[at].astype(F32)
-        for t in range(8):
-            path_ref[pl.ds(pl.multiple_of(8 * e, 8), 8), 128 * t : 128 * t + 128] = tile_ref[
-                pl.ds(t, 8, stride=8), :
-            ]
-        return 0
-
-    lax.fori_loop(0, path_ref.shape[0] // 8, link_group, 0)
     for store in stores:
         store.wait()
+
+
+def final_kernel(
+    tab_ref, link_hbm, grad_ref, head_ref, out_ref, path_ref, gh_ref,
+    link_ref, piece_ref, rows_ref, tile_ref, link_sem, in_sem, out_sem, path_sem,
+):
+    pieces = in_sem.shape[0]
+    links = path_ref.shape[0]
+    per = links // pieces
+    fetch = pltpu.make_async_copy(link_hbm, link_ref, link_sem)
+    fetch.start()
+    reads = load_chunks(grad_ref, piece_ref, in_sem)
+    for read in reads:
+        read.start()
+    gh_ref[...] = head_ref[...]
+    fetch.wait()
+    writes = []
+    for c in range(pieces):
+
+        for n in range(per // 8):
+            for j in range(8):
+                e = c * per // 8 + n
+                at = look_up(tab_ref, ROW_LINK + 2 * (j % 2), e * 4 + j // 2)
+                tile_ref[64 * n + 8 * j : 64 * n + 8 * j + 8, :] = link_ref[at].astype(F32)
+        for n in range(per // 8):
+            e = c * per // 8 + n
+            for t in range(8):
+                rows_ref[8 * e : 8 * e + 8, 128 * t : 128 * t + 128] = tile_ref[
+                    pl.ds(64 * n + t, 8, stride=8), :
+                ]
+        rows = pl.ds(c * per, per)
+        writes.append(pltpu.make_async_copy(rows_ref.at[rows], path_ref.at[rows], path_sem.at[c]))
+        writes[-1].start()
+        reads[c].wait()
+        cols = pl.ds(c * CHUNK, CHUNK)
+        writes.append(
+            pltpu.make_async_copy(piece_ref.at[:, cols], out_ref.at[:, cols], out_sem.at[c])
+        )
+        writes[-1].start()
+    for write in writes:
+        write.wait()
 
 
 def vmem():
@@ -660,11 +699,11 @@
     sem = pltpu.SemaphoreType.DMA
     heads = (paths * punits // 128, 128)
     tile = lambda n, width, kind: pltpu.VMEM((n, half, width), kind)
-    grad_gene, grad_pathway, grad_head = pl.pallas_call(
+    grad_parts, link_parts, head_parts = pl.pallas_call(
         functools.partial(main_kernel, devs, genes, units, paths, punits),
         out_shape=(
             shape((units, variants), F32),
-            shape((links, units * punits), F32),
+            shape((devs * CAP, half, 2 * punits), BF16),
             shape(heads, F32),
         ),
         in_specs=[smem()] + [vmem()] * 3 + [hbm()] * 2,
@@ -689,7 +728,6 @@
             tile(devs * HALF, 2 * punits, F32),
             tile(devs * HALF, 2 * punits, F32),
             tile(devs * CAP, 2 * samples, BF16),
-            tile(devs * CAP, 2 * punits, BF16),
             pltpu.VMEM((genes + 2, units, samples), BF16),
             pltpu.VMEM((genes + 2, units, samples), BF16),
             pltpu.VMEM((units, variants // 2), F32),
@@ -711,6 +749,28 @@
         genotypes,
         gene_weight,
     )
+    grad_gene, grad_pathway, grad_head = pl.pallas_call(
+        final_kernel,
+        out_shape=(
+            shape((units, variants), F32),
+            shape((links, units * punits), F32),
+            shape(heads, F32),
+        ),
+        in_specs=[smem(), hbm(), hbm(), vmem()],
+        out_specs=(hbm(), hbm(), vmem()),
+        scratch_shapes=[
+            pltpu.VMEM(link_parts.shape, BF16),
+            pltpu.VMEM((units, variants), F32),
+            pltpu.VMEM((links, units * punits), F32),
+            pltpu.VMEM((links // pieces * half, 2 * punits), F32),
+            sem(()),
+            sem((pieces,)),
+            sem((pieces,)),
+            sem((pieces,)),
+        ],
+        compiler_params=pltpu.CompilerParams(vmem_limit_bytes=LIMIT),
+        name="final",
+    )(tab, link_parts, grad_parts, head_parts)
     return grad_gene, grad_pathway, grad_head.reshape(-1)
 
 

time: 147 us -> 144 us (0.980)
  local copies, waits for them, and re-layouts: 5.62 us -> 0 us
  Pallas kernels: 140 us -> 143 us
    pallas_call x0 -> x1, Pallas kernels: none -> 6.75 us  [on_device(): pl.pallas_call(final_kernel, out_shape=(shape((units, variants), F32), sh...]
    unnamed x7 -> x0, local copies, waits for them, and re-layouts: 5.62 us -> none
    pallas_call x1, Pallas kernels: 131 us -> 127 us  [on_device(): pl.pallas_call(functools.partial(main_kernel, devs, genes, units, paths,...]
where the time goes in v4:
time: 144 us
  Pallas kernels  143 us (99%)
    pallas_call x1, Pallas kernels, on_device(): pl.pallas_call(functools.partial(main_kernel, devs, genes, units, paths,...  127 us
    pallas_call x1, Pallas kernels, on_device(): pl.pallas_call(functools.partial(index_kernel, devs, genes, paths), out_s...  9.18 us
    pallas_call x1, Pallas kernels, on_device(): pl.pallas_call(final_kernel, out_shape=(shape((units, variants), F32), sh...  6.75 us

profile of v4, /device:TPU:1, one launch (start us, length us, event | category | flops | bytes accessed | tf_op | source)
XLA Modules:
  0.0 143.9 jit_solution(4770346560556137105)
XLA Ops:
  0.6 9.2 %index.1 = (s32[80,128]{1,0:T(8,128)}, bf16[384,8,128]{2,1,0:T(8,128)(2,1)}) custom-call(s32[2,12288]{1,0:T(2,128)} %bitcast.6, s32[16,128]{1,0:T(8,128)} %bitcast.7, s32[1,192]{1,0:T(1,128)} %bitcast.9, bf16[384,1024]{1,0:T(8,128)(2,1)} %link_ref.1), custom_call_target="tpu_custom_call" | custom-call | tf_op jit(solution)/shard_map/index/pallas_call | solution.py:681
  9.8 127.3 %main.1 = (f32[16,49152]{1,0:T(8,128)}, bf16[768,8,128]{2,1,0:T(8,128)(2,1)}, f32[16,128]{1,0:T(8,128)}) custom-call(s32[80,128]{1,0:T(8,128)} %get-tuple-element.11.tab_ref, bf16[384,8,128]{2,1,0:T(8,128)(2,1)} %get-tuple-element.12.link_ref, bf16[16,128]{1,0:T(8,128)(2,1)} %bitcast.8, f32[1,128]{1,0:T(1,128)} %bitcast.10, bf16[128,49152]{1,0:T(8,128)(2,1)} %geno_ref.1, ...), custom_call_target="tpu_custom_call" | custom-call | tf_op jit(solution)/shard_map/main/pallas_call | solution.py:702
  137.1 6.7 %final.1 = (f32[16,49152]{1,0:T(8,128)}, f32[384,1024]{1,0:T(8,128)}, f32[16,128]{1,0:T(8,128)}) custom-call(s32[80,128]{1,0:T(8,128)} %get-tuple-element.11.tab_ref, bf16[768,8,128]{2,1,0:T(8,128)(2,1)} %get-tuple-element.13.link_hbm, f32[16,49152]{1,0:T(8,128)} %get-tuple-element.14.grad_ref, f32[16,128]{1,0:T(8,128)} %get-tuple-element.15.head_ref), custom_call_target="tpu_custom_call" | custom-call | tf_op jit(solution)/shard_map/final/pallas_call | solution.py:752

commit v5 on v4

--- a/solution.py
+++ b/solution.py
@@ -381,7 +381,7 @@
         ).start()
         return 0
 
-    lax.fori_loop(1, devs, h_step, 0)
+    lax.fori_loop(1, devs, h_step, 0, unroll=3)
     for r in range(CAP):
         h_ref[me * CAP + r] = hid_ref[tab_ref[r, me] >> 1]
     for r in range(HALF):
@@ -490,7 +490,7 @@
         ).start()
         return 0
 
-    lax.fori_loop(1, devs, d_step, 0)
+    lax.fori_loop(1, devs, d_step, 0, unroll=3)
 
     def down_links(i, _):
         for q in range(4):

time: 144 us -> 144 us (level)
  no operation moved by 1% of the time
where the time goes in v5:
time: 144 us
  Pallas kernels  143 us (99%)
    pallas_call x1, Pallas kernels, on_device(): pl.pallas_call(functools.partial(main_kernel, devs, genes, units, paths,...  127 us
    pallas_call x1, Pallas kernels, on_device(): pl.pallas_call(functools.partial(index_kernel, devs, genes, paths), out_s...  9.18 us
    pallas_call x1, Pallas kernels, on_device(): pl.pallas_call(final_kernel, out_shape=(shape((units, variants), F32), sh...  6.75 us

profile of v5, /device:TPU:1, one launch (start us, length us, event | category | flops | bytes accessed | tf_op | source)
XLA Modules:
  0.0 144.0 jit_solution(2124024580102235034)
XLA Ops:
  0.6 9.2 %index.1 = (s32[80,128]{1,0:T(8,128)}, bf16[384,8,128]{2,1,0:T(8,128)(2,1)}) custom-call(s32[2,12288]{1,0:T(2,128)} %bitcast.6, s32[16,128]{1,0:T(8,128)} %bitcast.7, s32[1,192]{1,0:T(1,128)} %bitcast.9, bf16[384,1024]{1,0:T(8,128)(2,1)} %link_ref.1), custom_call_target="tpu_custom_call" | custom-call | tf_op jit(solution)/shard_map/index/pallas_call | solution.py:681
  9.8 127.4 %main.1 = (f32[16,49152]{1,0:T(8,128)}, bf16[768,8,128]{2,1,0:T(8,128)(2,1)}, f32[16,128]{1,0:T(8,128)}) custom-call(s32[80,128]{1,0:T(8,128)} %get-tuple-element.11.tab_ref, bf16[384,8,128]{2,1,0:T(8,128)(2,1)} %get-tuple-element.12.link_ref, bf16[16,128]{1,0:T(8,128)(2,1)} %bitcast.8, f32[1,128]{1,0:T(1,128)} %bitcast.10, bf16[128,49152]{1,0:T(8,128)(2,1)} %geno_ref.1, ...), custom_call_target="tpu_custom_call" | custom-call | tf_op jit(solution)/shard_map/main/pallas_call | solution.py:702
  137.2 6.7 %final.1 = (f32[16,49152]{1,0:T(8,128)}, f32[384,1024]{1,0:T(8,128)}, f32[16,128]{1,0:T(8,128)}) custom-call(s32[80,128]{1,0:T(8,128)} %get-tuple-element.11.tab_ref, bf16[768,8,128]{2,1,0:T(8,128)(2,1)} %get-tuple-element.13.link_hbm, f32[16,49152]{1,0:T(8,128)} %get-tuple-element.14.grad_ref, f32[16,128]{1,0:T(8,128)} %get-tuple-element.15.head_ref), custom_call_target="tpu_custom_call" | custom-call | tf_op jit(solution)/shard_map/final/pallas_call | solution.py:752
